TPU v7x, 512 devices: a whole 4x4x16 slice. The times are simulated.
512 devices in a mesh: dom: 64 (over z, y), tp: 8 (over x, core).
Axes of the slice: x: 4, y: 4, z: 16, core: 2. Of those that a mesh axis runs over, the one named last changes fastest.
Arguments:
- queries: bfloat16 [2, 1024, 8192], P(None, 'dom', 'tp'), may hold values from -400 to 400
- new_kv: bfloat16 [2, 1024, 2048], P(None, 'dom', 'tp'), may hold values from -5 to 5
- gen_cache: bfloat16 [1024, 128, 2048], P('dom', None, 'tp'), may hold values from -5 to 5
- prompt_kv: bfloat16 [4096, 2048], P(None, 'tp'), may hold values from -5 to 5
- lengths: int32 [1024], replicated, may hold values from 1 to 126
- ancestors: int32 [1024], replicated, may hold values from 0 to 1023, as said below
- tokens: int32 [2, 1024], P(None, 'dom'), may hold values from 0 to 128255
- twist_vector: float32 [8192], P('tp'), may hold values from -31 to 31
- twist_bias: float32 [128256], replicated, may hold values from -5 to 5
- prior_weights: float32 [1024], P('dom'), may hold values from -252 to 4
Outputs:
- twist: float32 [2, 1024], P(None, 'dom')
- normalized: float32 [1024], P('dom')
- resampled_cache: bfloat16 [1024, 128, 2048], P('dom', None, 'tp')
- new_lengths: int32 [1024], P('dom')
Inputs may be any that keep to these rules, and one draw needn't show every extreme that they name: Particle p's ancestor lies on the index of dom that holds p or at most 2 indices from it; the particles of one index of dom name at most 2 distinct ancestors on any other index, and exactly 2 for some pair of indices.
All inputs are finite; a program needn't handle non-finite values.
Results may differ from a plain program's by a relative error of at most 0.0018.
Values may be sent and summed in bfloat16 or wider, within the bound.
A program may use at most 64 MiB of HBM per device.

v0:
```python
import math

import jax
import jax.numpy as jnp
from jax import lax
from jax.sharding import PartitionSpec as P

HEAD_DIM = 128
SPAN = 2


NEG_FILL = -1e30


def shifted(block, axis, distance):
    devices = range(lax.axis_size(axis))
    route = [(i - distance, i) for i in devices if i - distance in devices]
    return lax.ppermute(block, axis, route)


def grow_cache(gen_cache, new_kv, own_lengths):
    slot_ids = lax.broadcasted_iota(jnp.int32, (1, gen_cache.shape[1], 1), 1)
    start_row = own_lengths[:, None, None]
    first_row = new_kv[0][:, None, :]
    second = new_kv[1][:, None, :]
    empty_rows = jnp.zeros_like(gen_cache)
    later_rows = jnp.where(slot_ids == start_row + 1, second, empty_rows)
    return jnp.where(
        slot_ids < start_row, gen_cache, jnp.where(slot_ids == start_row, first_row, later_rows)
    )


def attend(queries, prompt_kv, grown, own_lengths):
    step_count, per_dev, width = queries.shape
    kv_local = prompt_kv.shape[1] // (2 * HEAD_DIM)
    group_size = width // (kv_local * HEAD_DIM)
    query_heads = queries.reshape(step_count, per_dev, kv_local, group_size, HEAD_DIM)
    prompt = prompt_kv.reshape(prompt_kv.shape[0], kv_local, 2, HEAD_DIM)
    cached = grown.reshape(per_dev, grown.shape[1], kv_local, 2, HEAD_DIM)
    score_scale = 1.0 / math.sqrt(HEAD_DIM)
    prompt_scores = (
        jnp.einsum(
            "tpcgd,scd->tpcgs", query_heads, prompt[:, :, 0], preferred_element_type=jnp.float32
        )
        * score_scale
    )
    cache_scores = (
        jnp.einsum(
            "tpcgd,pscd->tpcgs", query_heads, cached[:, :, :, 0], preferred_element_type=jnp.float32
        )
        * score_scale
    )
    slot_ids = lax.broadcasted_iota(jnp.int32, (step_count, 1, 1, 1, grown.shape[1]), 4)
    step_ids = lax.broadcasted_iota(jnp.int32, (step_count, 1, 1, 1, 1), 0)
    visible = slot_ids <= own_lengths[None, :, None, None, None] + step_ids
    cache_scores = jnp.where(visible, cache_scores, NEG_FILL)
    row_max = jnp.maximum(
        jnp.max(prompt_scores, axis=-1, keepdims=True),
        jnp.max(cache_scores, axis=-1, keepdims=True),
    )
    prompt_exp = jnp.exp(prompt_scores - row_max)
    cache_exp = jnp.where(visible, jnp.exp(cache_scores - row_max), 0.0)
    row_sum = jnp.sum(prompt_exp, axis=-1) + jnp.sum(cache_exp, axis=-1)
    mixed = jnp.einsum(
        "tpcgs,scd->tpcgd",
        prompt_exp.astype(jnp.bfloat16),
        prompt[:, :, 1],
        preferred_element_type=jnp.float32,
    )
    mixed = mixed + jnp.einsum(
        "tpcgs,pscd->tpcgd",
        cache_exp.astype(jnp.bfloat16),
        cached[:, :, :, 1],
        preferred_element_type=jnp.float32,
    )
    return mixed / row_sum[..., None]


def local(
    queries,
    new_kv,
    gen_cache,
    prompt_kv,
    lengths,
    ancestors,
    tokens,
    twist_vector,
    twist_bias,
    prior_weights,
):
    per_dev = gen_cache.shape[0]
    own_index = lax.axis_index("dom")
    own_lengths = lax.dynamic_slice_in_dim(lengths, own_index * per_dev, per_dev)
    own_anc = lax.dynamic_slice_in_dim(ancestors, own_index * per_dev, per_dev)
    grown = grow_cache(gen_cache, new_kv, own_lengths)
    mixed = attend(queries, prompt_kv, grown, own_lengths)
    head_weights = twist_vector.reshape(mixed.shape[2:])
    partial_twist = jnp.sum(mixed * head_weights, axis=(2, 3, 4))
    twist = lax.psum(partial_twist, "tp") + jnp.take(twist_bias, tokens, axis=0)
    log_weight = prior_weights + twist[1] - twist[0]
    largest = lax.pmax(jnp.max(log_weight), "dom")
    exp_total = lax.psum(jnp.sum(jnp.exp(log_weight - largest)), "dom")
    normalized = log_weight - (largest + jnp.log(exp_total))
    flat_cache = grown.reshape(per_dev, -1)
    local_ids = lax.broadcasted_iota(jnp.int32, (1, per_dev), 1)
    home_pick = (own_anc[:, None] == own_index * per_dev + local_ids).astype(jnp.bfloat16)
    moved = jnp.dot(home_pick, flat_cache, preferred_element_type=jnp.float32)
    offsets = [shift_by for shift_by in range(-SPAN, SPAN + 1) if shift_by != 0]
    for shift_by in offsets:
        incoming = shifted(flat_cache, "dom", shift_by)
        picker = (own_anc[:, None] == (own_index - shift_by) * per_dev + local_ids).astype(
            jnp.bfloat16
        )
        moved = moved + jnp.dot(picker, incoming, preferred_element_type=jnp.float32)
    resampled_cache = moved.reshape(gen_cache.shape).astype(jnp.bfloat16)
    new_lengths = jnp.take(lengths, own_anc, axis=0) + 2
    return (twist, normalized, resampled_cache, new_lengths)


def solution(mesh):
    in_specs = (
        P(None, "dom", "tp"),
        P(None, "dom", "tp"),
        P("dom", None, "tp"),
        P(None, "tp"),
        P(),
        P(),
        P(None, "dom"),
        P("tp"),
        P(),
        P("dom"),
    )
    out_specs = (P(None, "dom"), P("dom"), P("dom", None, "tp"), P("dom"))
    return jax.shard_map(local, mesh=mesh, in_specs=in_specs, out_specs=out_specs, check_vma=False)
```

profile of v0, /device:TPU:388, one launch (start us, length us, event | category | flops | bytes accessed | tf_op | source)
XLA Modules:
  0.0 380.1 jit_solution(7351187828314626756)
XLA Ops:
  0.7 1.7 copy.56
  2.5 1.2 select_select_fusion
  3.8 1.7 copy.76
  5.5 5.1 %collective-permute-start.3 = (bf16[16,32768]{1,0:T(8,128)(2,1)}, bf16[16,32768]{1,0:T(8,128)(2,1)}, u32[]{:S(2)}, u32[]{:S(2)}) collective-permute-start(bf16[16,32768]{1,0:T(8,128)(2,1)} %bitcast.54), channel_id=1, source_target_pairs={{0,16},{8,24},{16,32},{24,40},{32,48},{40,56},{48,64},{56,72},{64,... | collective-permute-start | bytes 3145736 | tf_op jit(solution)/shard_map/ppermute | solution.py:18
  10.6 2.6 collective-permute-start.2
  13.2 5.9 %collective-permute-start = (bf16[16,32768]{1,0:T(8,128)(2,1)}, bf16[16,32768]{1,0:T(8,128)(2,1)}, u32[]{:S(2)}, u32[]{:S(2)}) collective-permute-start(bf16[16,32768]{1,0:T(8,128)(2,1)} %bitcast.54), channel_id=1, source_target_pairs={{16,0},{24,8},{32,16},{40,24},{48,32},{56,40},{64,48},{72,56},{80,... | collective-permute-start | bytes 3145736 | tf_op jit(solution)/shard_map/ppermute | solution.py:18
  19.1 2.6 collective-permute-start.1
  21.8 2.9 copy.53
  24.9 2.6 fusion.60
  28.0 1.5 fusion.27
  29.7 2.9 fusion.4
  32.7 3.1 fusion.24
  35.9 10.8 %psum.14 = f32[2,16]{1,0:T(2,128)S(1)} all-reduce(f32[2,16]{1,0:T(2,128)S(1)} %fusion.24), channel_id=1, replica_groups=mesh['dom'=64,'tp'=8] {'tp'}, use_global_device_ids=true, to_apply=%region_5.6 | all-reduce | flops 32 | bytes 256 | tf_op jit(solution)/shard_map/psum | solution.py:99
  46.8 0.7 gather_fusion
  48.2 176.0 %pmax.7 = f32[]{:T(128)} all-reduce(f32[]{:T(128)} %get-tuple-element.6), channel_id=1, replica_groups=mesh['dom'=64,'tp'=8] {'dom'}, use_global_device_ids=true, to_apply=%region_7.8 | all-reduce | flops 1 | bytes 8 | tf_op jit(solution)/shard_map/pmax | solution.py:101
  224.2 1.2 exponential_reduce_fusion
  225.5 140.9 %psum.15 = f32[]{:T(128)} all-reduce(f32[]{:T(128)} %exponential_reduce_fusion), channel_id=1, replica_groups=mesh['dom'=64,'tp'=8] {'dom'}, use_global_device_ids=true, to_apply=%region_9.10 | all-reduce | flops 1 | bytes 8 | tf_op jit(solution)/shard_map/psum | solution.py:102
  367.7 0.8 compare_select_fusion.1
  370.1 1.7 fusion.44
  371.8 1.7 fusion.38
  373.6 1.7 fusion.40
  375.3 1.7 convolution_add_fusion.1
  377.1 1.8 fusion.2
  378.9 1.2 copy.77
  (51 shorter events, 3.7 us)
Async XLA Ops:
  0.6 46.1 %copy-start = (f32[128256]{0:T(1024)S(1)}, f32[128256]{0:T(1024)}, u32[]{:S(2)}) copy-start(f32[128256]{0:T(1024)} %param.18) | copy-start | bytes 1539076
  0.6 1.7 copy-start.6
  0.7 1.7 copy-start.1
  3.8 17.9 %copy-start.2 = (bf16[16,128,256]{1,2,0:T(8,128)(2,1)}, bf16[16,128,256]{1,2,0:T(8,128)(2,1)S(1)}, u32[]{:S(2)}) copy-start(bf16[16,128,256]{1,2,0:T(8,128)(2,1)S(1)} %select_select_fusion) | copy-start | bytes 3145732
  5.5 366.3 %collective-permute-start.3 = (bf16[16,32768]{1,0:T(8,128)(2,1)}, bf16[16,32768]{1,0:T(8,128)(2,1)}, u32[]{:S(2)}, u32[]{:S(2)}) collective-permute-start(bf16[16,32768]{1,0:T(8,128)(2,1)} %bitcast.54), channel_id=1, source_target_pairs={{0,16},{8,24},{16,32},{24,40},{32,48},{40,56},{48,64},{56,72},{64,... | collective-permute-start | bytes 3145736 | tf_op jit(solution)/shard_map/ppermute | solution.py:18
  10.6 363.0 %collective-permute-start.2 = (bf16[16,32768]{1,0:T(8,128)(2,1)}, bf16[16,32768]{1,0:T(8,128)(2,1)}, u32[]{:S(2)}, u32[]{:S(2)}) collective-permute-start(bf16[16,32768]{1,0:T(8,128)(2,1)} %bitcast.54), channel_id=1, source_target_pairs={{0,8},{8,16},{16,24},{24,32},{32,40},{40,48},{48,56},{56,64},{64,7... | collective-permute-start | bytes 3145736 | tf_op jit(solution)/shard_map/ppermute | solution.py:18
  13.2 362.1 %collective-permute-start = (bf16[16,32768]{1,0:T(8,128)(2,1)}, bf16[16,32768]{1,0:T(8,128)(2,1)}, u32[]{:S(2)}, u32[]{:S(2)}) collective-permute-start(bf16[16,32768]{1,0:T(8,128)(2,1)} %bitcast.54), channel_id=1, source_target_pairs={{16,0},{24,8},{32,16},{40,24},{48,32},{56,40},{64,48},{72,56},{80,... | collective-permute-start | bytes 3145736 | tf_op jit(solution)/shard_map/ppermute | solution.py:18
  19.1 358.0 %collective-permute-start.1 = (bf16[16,32768]{1,0:T(8,128)(2,1)}, bf16[16,32768]{1,0:T(8,128)(2,1)}, u32[]{:S(2)}, u32[]{:S(2)}) collective-permute-start(bf16[16,32768]{1,0:T(8,128)(2,1)} %bitcast.54), channel_id=1, source_target_pairs={{8,0},{16,8},{24,16},{32,24},{40,32},{48,40},{56,48},{64,56},{72,6... | collective-permute-start | bytes 3145736 | tf_op jit(solution)/shard_map/ppermute | solution.py:18
  21.8 3.0 copy-start.4
  24.8 2.7 copy-start.3
  29.7 3.0 copy-start.5
  32.7 14.0 %copy-start.7 = (s32[2,16]{1,0:T(2,128)S(1)}, s32[2,16]{1,0:T(2,128)}, u32[]{:S(2)}) copy-start(s32[2,16]{1,0:T(2,128)} %param.16) | copy-start | bytes 388
  32.7 14.9 %copy-start.9 = (f32[16]{0:T(128)S(1)}, f32[16]{0:T(128)}, u32[]{:S(2)}) copy-start(f32[16]{0:T(128)} %param.19) | copy-start | bytes 196
  47.6 326.0 %copy-start.8 = (f32[2,16]{1,0:T(2,128)}, f32[2,16]{1,0:T(2,128)S(1)}, u32[]{:S(2)}) copy-start(f32[2,16]{1,0:T(2,128)S(1)} %fusion.56) | copy-start | bytes 388
where the time goes:
time: 381 us; the launch traced here: 380 us
  blocking collectives  328 us (86%)
  matrix products  16.3 us (4%)
  starting transfers between devices  16.2 us (4%)
  local copies, waits for them, and re-layouts  9.34 us (2%)
  other arithmetic  8.36 us (2%)
    pmax x1, blocking collectives, local(): largest = lax.pmax(jnp.max(log_weight), 'dom')  176 us
    psum x1, blocking collectives, local(): exp_total = lax.psum(jnp.sum(jnp.exp(log_weight - largest)), 'dom')  141 us
    ppermute x4, starting transfers between devices, shifted(): return lax.ppermute(block, axis, route)  16.2 us
    psum x1, blocking collectives, local(): twist = lax.psum(partial_twist, 'tp') + jnp.take(twist_bias, tokens, axis=0)  10.8 us
  transfers between devices with their start and end apart: 4, of which 0 were waited for; matrix products, arithmetic and copies ran while one was open for 7% of the time, Pallas kernels for 0%

commit v1 on v0

v1 whole, which is shorter than its diff:
```python
import functools
import math

import jax
import jax.numpy as jnp
from jax import lax
from jax.experimental import pallas as pl
from jax.experimental.pallas import tpu as pltpu
from jax.sharding import PartitionSpec as P

HEAD_DIM = 128
Y_DIM = 4
NEG_FILL = -1e30
MESH = pl.DeviceIdType.MESH
LOG2E = 1.4426950408889634
OFFSETS = (2, 1, -2, -1)


def kernel(
    sizes,
    anc,
    lens,
    toks,
    prior,
    q_hbm,
    new_hbm,
    gen_hbm,
    prompt_hbm,
    tv_ref,
    bias_hbm,
    twist_out,
    norm_out,
    cache_out,
    len_out,
    qv,
    newv,
    cache,
    keyv,
    valv,
    biasv,
    scores,
    picked,
    relay,
    landed,
    outv,
    bias_rows,
    plane_rows,
    z_rows,
    in_sems,
    out_sem,
    hop_send,
    hop_recv,
    plane_send,
    plane_recv,
    z_send,
    z_recv,
):
    n_dom, n_tp, per_dev, gen, prompt_len, group = sizes
    n_z = n_dom // Y_DIM
    n_plane = n_tp * Y_DIM
    dom = lax.axis_index("dom")
    tp = lax.axis_index("tp")
    my_y = lax.rem(dom, Y_DIM)
    my_z = dom // Y_DIM
    base = dom * per_dev

    def device(d, t):
        return {"dom": d, "tp": t}

    after = lax.rem(dom + 1, n_dom)
    before = lax.rem(dom + n_dom - 1, n_dom)

    def plane_peer(k):
        slot = lax.rem(tp * Y_DIM + my_y + k, n_plane)
        return slot, device(my_z * Y_DIM + lax.rem(slot, Y_DIM), slot // Y_DIM)

    def z_peer(k):
        slot = lax.rem(my_z + k, n_z)
        return slot, device(slot * Y_DIM + my_y, tp)

    def load(src, dst, i):
        return pltpu.make_async_copy(src, dst, in_sems.at[i])

    loads = [
        load(gen_hbm, cache, 0),
        load(new_hbm, newv, 1),
        load(q_hbm, qv, 2),
        load(prompt_hbm.at[:, 0:HEAD_DIM], keyv, 3),
        load(prompt_hbm.at[:, HEAD_DIM : 2 * HEAD_DIM], valv, 4),
        load(bias_hbm, biasv, 5),
    ]
    for item in loads:
        item.start()

    barrier = pltpu.get_barrier_semaphore()
    for d in (after, before):
        pl.semaphore_signal(barrier, inc=1, device_id=device(d, tp), device_id_type=MESH)

    def greet_plane(k, carry):
        pl.semaphore_signal(barrier, inc=1, device_id=plane_peer(k)[1], device_id_type=MESH)
        return carry

    def greet_z(k, carry):
        pl.semaphore_signal(barrier, inc=1, device_id=z_peer(k)[1], device_id_type=MESH)
        return carry

    lax.fori_loop(1, n_plane, greet_plane, 0)
    lax.fori_loop(1, n_z, greet_z, 0)

    for p in range(per_dev):
        len_out[p] = lens[anc[base + p]] + 2

    loads[0].wait()
    loads[1].wait()
    rows = lax.broadcasted_iota(jnp.int32, (gen, 2 * HEAD_DIM), 0)

    def grow(p, carry):
        start = lens[base + p]
        first = newv[0, pl.ds(p, 1), :].astype(jnp.float32)
        second = newv[1, pl.ds(p, 1), :].astype(jnp.float32)
        kept = cache[p].astype(jnp.float32)
        later = jnp.where(rows == start + 1, second, 0.0)
        grown = jnp.where(rows < start, kept, jnp.where(rows == start, first, later))
        cache[p] = grown.astype(jnp.bfloat16)
        return carry

    for p in range(per_dev):
        grow(p, 0)

    for slot, offset in enumerate(OFFSETS):
        target = lax.rem(dom + offset + n_dom, n_dom) * per_dev
        low, high = per_dev - 1, 0
        for i in range(per_dev):
            spot = anc[target + i] - base
            mine = jnp.logical_and(spot >= 0, spot < per_dev)
            low = jnp.minimum(low, jnp.where(mine, spot, per_dev - 1))
            high = jnp.maximum(high, jnp.where(mine, spot, 0))
        picked[slot, 0] = cache[low]
        picked[slot, 1] = cache[high]

    pl.semaphore_wait(barrier, 2 + n_plane - 1 + n_z - 1)

    def hop(src, dst, i, d):
        return pltpu.make_async_remote_copy(
            src_ref=src,
            dst_ref=dst,
            send_sem=hop_send.at[i],
            recv_sem=hop_recv.at[i],
            device_id=device(d, tp),
            device_id_type=MESH,
        )

    hops = [
        hop(picked.at[0], relay.at[0], 0, after),
        hop(picked.at[2], relay.at[1], 1, before),
        hop(picked.at[1], landed.at[1], 2, after),
        hop(picked.at[3], landed.at[3], 3, before),
        hop(relay.at[0], landed.at[0], 4, after),
        hop(relay.at[1], landed.at[2], 5, before),
    ]
    for item in hops[:4]:
        item.start()

    n_rows = 2 * group * per_dev
    loads[2].wait()
    tiles = [qv[t, :, h * HEAD_DIM : (h + 1) * HEAD_DIM] for t in range(2) for h in range(group)]
    stacked = jnp.concatenate(tiles, axis=0)
    to_row = lax.broadcasted_iota(jnp.int32, (n_rows, n_rows), 0)
    from_row = lax.broadcasted_iota(jnp.int32, (n_rows, n_rows), 1)
    wanted = lax.rem(to_row, 2 * group) * per_dev + to_row // (2 * group)
    order = jnp.where(from_row == wanted, 1.0, 0.0).astype(jnp.bfloat16)
    query = jnp.dot(order, stacked, preferred_element_type=jnp.float32).astype(jnp.bfloat16)

    nt = (((1,), (1,)), ((), ()))
    part = 2 * group
    own = []
    cols = lax.broadcasted_iota(jnp.int32, (part, gen), 1)
    step = lax.broadcasted_iota(jnp.int32, (part, gen), 0) // group
    for p in range(per_dev):
        raw = lax.dot_general(
            query[p * part : (p + 1) * part], cache[p, :, 0:HEAD_DIM], nt,
            preferred_element_type=jnp.float32,
        )
        own.append(jnp.where(cols <= lens[base + p] + step, raw, NEG_FILL))
    own = jnp.concatenate(own, axis=0)
    top = own
    loads[3].wait()
    chunk = 512
    for c in range(prompt_len // chunk):
        raw = lax.dot_general(
            query, keyv[c * chunk : (c + 1) * chunk, :], nt, preferred_element_type=jnp.float32
        )
        scores[:, c * chunk : (c + 1) * chunk] = raw
        for i in range(chunk // 128):
            top = jnp.maximum(top, raw[:, i * 128 : (i + 1) * 128])
    row_max = jnp.max(top, axis=1, keepdims=True)
    scale = LOG2E / math.sqrt(HEAD_DIM)
    exps = jnp.exp2((own - row_max) * scale)
    total = exps
    probs = exps.astype(jnp.bfloat16)
    mixed = []
    for p in range(per_dev):
        mixed.append(
            jnp.dot(
                probs[p * part : (p + 1) * part], cache[p, :, HEAD_DIM : 2 * HEAD_DIM],
                preferred_element_type=jnp.float32,
            )
        )
    mixed = jnp.concatenate(mixed, axis=0)
    loads[4].wait()
    for c in range(prompt_len // chunk):
        exps = jnp.exp2((scores[:, c * chunk : (c + 1) * chunk] - row_max) * scale)
        for i in range(chunk // 128):
            total = total + exps[:, i * 128 : (i + 1) * 128]
        mixed = mixed + jnp.dot(
            exps.astype(jnp.bfloat16), valv[c * chunk : (c + 1) * chunk, :],
            preferred_element_type=jnp.float32,
        )
    row_sum = jnp.sum(total, axis=1, keepdims=True)
    mixed = mixed / row_sum
    weighted = mixed.reshape(2 * per_dev, group, HEAD_DIM) * tv_ref[...][None]
    pair_rows = jnp.sum(weighted, axis=1)

    loads[5].wait()
    lanes = lax.broadcasted_iota(jnp.int32, (1, 128), 1)
    for p in range(per_dev):
        for t in range(2):
            token = toks[t, p]
            row = biasv[pl.ds(token // 128, 1), :]
            bias_rows[p * 2 + t : p * 2 + t + 1, :] = jnp.where(lanes == lax.rem(token, 128), row, 0.0)
    first_tp = jnp.where(tp == 0, 1.0, 0.0)
    pair_rows = pair_rows + bias_rows[...] * first_tp
    pair_col = jnp.sum(pair_rows, axis=1, keepdims=True)
    pair_ids = lax.broadcasted_iota(jnp.int32, (2 * per_dev, 128), 0)
    lane_ids = lax.broadcasted_iota(jnp.int32, (2 * per_dev, 128), 1)
    at_lane = lane_ids == lax.rem(pair_ids, 2) * per_dev + pair_ids // 2
    message = jnp.sum(jnp.where(at_lane, pair_col, 0.0), axis=0, keepdims=True)
    for p in range(per_dev):
        message = jnp.where(lanes == 2 * per_dev + p, prior[p] * first_tp, message)

    me = tp * Y_DIM + my_y
    plane_rows[me] = message

    def plane_copy(src, dst, peer):
        return pltpu.make_async_remote_copy(
            src_ref=plane_rows.at[src],
            dst_ref=plane_rows.at[dst],
            send_sem=plane_send.at[peer[0]],
            recv_sem=plane_recv.at[dst],
            device_id=peer[1],
            device_id_type=MESH,
        )

    def plane_start(k, carry):
        plane_copy(me, me, plane_peer(k)).start()
        return carry

    lax.fori_loop(1, n_plane, plane_start, 0)

    hops[0].wait_recv()
    hops[4].start()
    hops[1].wait_recv()
    hops[5].start()

    def plane_wait(k, carry):
        peer = plane_peer(k)
        plane_copy(me, peer[0], peer).wait()
        return carry

    lax.fori_loop(1, n_plane, plane_wait, 0)

    def summed(y):
        acc = plane_rows[y]
        for t in range(1, n_tp):
            acc = acc + plane_rows[t * Y_DIM + y]
        return acc

    def weights(acc):
        later = pltpu.roll(acc, 128 - per_dev, 1)
        given = pltpu.roll(acc, 128 - 2 * per_dev, 1)
        return jnp.where(lanes < per_dev, given + later - acc, NEG_FILL), later

    own_sum = summed(my_y)
    own_weight, own_later = weights(own_sum)
    twist_out[0:1, :] = own_sum[:, 0:per_dev]
    twist_out[1:2, :] = own_later[:, 0:per_dev]
    all_weights = jnp.concatenate([weights(summed(y))[0] for y in range(Y_DIM)], axis=0)
    z_max = jnp.max(jnp.max(all_weights, axis=1, keepdims=True), axis=0, keepdims=True)
    z_exp = jnp.exp(all_weights - z_max)
    z_sum = jnp.sum(jnp.sum(z_exp, axis=1, keepdims=True), axis=0, keepdims=True)
    z_rows[my_z, 0:1, :] = jnp.broadcast_to(z_max, (1, 128))
    z_rows[my_z, 1:2, :] = jnp.broadcast_to(z_sum, (1, 128))

    def z_copy(dst, peer):
        return pltpu.make_async_remote_copy(
            src_ref=z_rows.at[my_z],
            dst_ref=z_rows.at[dst],
            send_sem=z_send.at[peer[0]],
            recv_sem=z_recv.at[dst],
            device_id=peer[1],
            device_id_type=MESH,
        )

    def z_start(k, carry):
        z_copy(my_z, z_peer(k)).start()
        return carry

    lax.fori_loop(1, n_z, z_start, 0)

    for item in hops[2:]:
        item.wait_recv()
    firsts = []
    for offset in OFFSETS:
        low = per_dev - 1
        for i in range(per_dev):
            spot = anc[base + i] - (base - offset * per_dev)
            theirs = jnp.logical_and(spot >= 0, spot < per_dev)
            low = jnp.minimum(low, jnp.where(theirs, spot, per_dev - 1))
        firsts.append(low)
    for p in range(per_dev):
        spot = anc[base + p] - base
        home = jnp.logical_and(spot >= 0, spot < per_dev)
        home_spot = jnp.clip(spot, 0, per_dev - 1)
        place = 0
        for slot, offset in enumerate(OFFSETS):
            there = spot + offset * per_dev
            theirs = jnp.logical_and(there >= 0, there < per_dev)
            second = jnp.where(there == firsts[slot], 0, 1)
            place = jnp.where(theirs, 2 * slot + second, place)
        moved = landed[place // 2, lax.rem(place, 2)]
        outv[p] = jnp.where(home, cache[home_spot], moved)
    written = pltpu.make_async_copy(outv, cache_out, out_sem)
    written.start()

    def z_wait(k, carry):
        peer = z_peer(k)
        z_copy(peer[0], peer).wait()
        return carry

    lax.fori_loop(1, n_z, z_wait, 0)
    maxes = z_rows[:, 0, :]
    sums = z_rows[:, 1, :]
    largest = jnp.max(maxes, axis=0, keepdims=True)
    exp_total = jnp.sum(sums * jnp.exp(maxes - largest), axis=0, keepdims=True)
    normalized = own_weight - (largest + jnp.log(exp_total))
    norm_out[...] = normalized[:, 0:per_dev]

    for item in hops:
        item.wait_send()
    written.wait()


def local(
    n_dom,
    n_tp,
    queries,
    new_kv,
    gen_cache,
    prompt_kv,
    lengths,
    ancestors,
    tokens,
    twist_vector,
    twist_bias,
    prior_weights,
):
    per_dev, gen, width = gen_cache.shape
    prompt_len = prompt_kv.shape[0]
    group = queries.shape[2] // HEAD_DIM
    n_rows = 2 * group * per_dev
    n_z = n_dom // Y_DIM
    n_plane = n_tp * Y_DIM
    any_space = pl.BlockSpec(memory_space=pl.ANY)
    smem = pl.BlockSpec(memory_space=pltpu.SMEM)
    vmem = pl.BlockSpec(memory_space=pltpu.VMEM)
    f32, bf16 = jnp.float32, jnp.bfloat16
    twist, normalized, resampled, new_lengths = pl.pallas_call(
        functools.partial(kernel, (n_dom, n_tp, per_dev, gen, prompt_len, group)),
        out_shape=(
            jax.ShapeDtypeStruct((2, per_dev), f32),
            jax.ShapeDtypeStruct((1, per_dev), f32),
            jax.ShapeDtypeStruct(gen_cache.shape, bf16),
            jax.ShapeDtypeStruct((per_dev,), jnp.int32),
        ),
        in_specs=[smem] * 4 + [any_space] * 4 + [vmem, any_space],
        out_specs=(vmem, vmem, any_space, smem),
        scratch_shapes=[
            pltpu.VMEM(queries.shape, bf16),
            pltpu.VMEM(new_kv.shape, bf16),
            pltpu.VMEM(gen_cache.shape, bf16),
            pltpu.VMEM((prompt_len, HEAD_DIM), bf16),
            pltpu.VMEM((prompt_len, HEAD_DIM), bf16),
            pltpu.VMEM((twist_bias.shape[0] // 128, 128), f32),
            pltpu.VMEM((n_rows, prompt_len), f32),
            pltpu.VMEM((4, 2, gen, width), bf16),
            pltpu.VMEM((2, 2, gen, width), bf16),
            pltpu.VMEM((4, 2, gen, width), bf16),
            pltpu.VMEM(gen_cache.shape, bf16),
            pltpu.VMEM((2 * per_dev, 128), f32),
            pltpu.VMEM((n_plane, 1, 128), f32),
            pltpu.VMEM((n_z, 2, 128), f32),
            pltpu.SemaphoreType.DMA((6,)),
            pltpu.SemaphoreType.DMA,
            pltpu.SemaphoreType.DMA((6,)),
            pltpu.SemaphoreType.DMA((6,)),
            pltpu.SemaphoreType.DMA((n_plane,)),
            pltpu.SemaphoreType.DMA((n_plane,)),
            pltpu.SemaphoreType.DMA((n_z,)),
            pltpu.SemaphoreType.DMA((n_z,)),
        ],
        compiler_params=pltpu.CompilerParams(collective_id=0, has_side_effects=True),
        name="smc_step",
    )(
        ancestors,
        lengths,
        tokens,
        prior_weights,
        queries,
        new_kv,
        gen_cache,
        prompt_kv,
        twist_vector.reshape(group, HEAD_DIM),
        twist_bias.reshape(-1, 128),
    )
    return twist, normalized.reshape(per_dev), resampled, new_lengths


def solution(mesh):
    in_specs = (
        P(None, "dom", "tp"),
        P(None, "dom", "tp"),
        P("dom", None, "tp"),
        P(None, "tp"),
        P(),
        P(),
        P(None, "dom"),
        P("tp"),
        P(),
        P("dom"),
    )
    out_specs = (P(None, "dom"), P("dom"), P("dom", None, "tp"), P("dom"))
    return jax.shard_map(
        functools.partial(local, mesh.shape["dom"], mesh.shape["tp"]),
        mesh=mesh,
        in_specs=in_specs,
        out_specs=out_specs,
        check_vma=False,
    )
```

time: 381 us -> 40.5 us (0.11)
  the two profiles are of different devices: /device:TPU:388 before, /device:TPU:1 now
where the time goes in v1:
time: 40.5 us; the launch traced here: 40.3 us
  Pallas kernels  34.4 us (85%)
  local copies, waits for them, and re-layouts  5.2 us (13%)
  between operations  0.65 us (2%)
    pallas_call x1, Pallas kernels, local(): pl.pallas_call(functools.partial(kernel, (n_dom, n_tp, per_dev, gen, prom...  34.4 us
    unnamed x6, local copies, waits for them, and re-layouts  5.2 us

profile of v1, /device:TPU:1, one launch (start us, length us, event | category | flops | bytes accessed | tf_op | source)
XLA Modules:
  0.0 40.3 jit_solution(3245350564684943397)
XLA Ops:
  0.6 34.4 %smc_step.1 = (f32[2,16]{1,0:T(2,128)}, f32[1,16]{1,0:T(1,128)}, bf16[16,128,256]{2,1,0:T(8,128)(2,1)}, s32[16]{0:T(128)}) custom-call(s32[1024]{0:T(1024)} %anc.1, s32[1024]{0:T(1024)} %lens.1, s32[2,16]{1,0:T(2,128)} %toks.1, f32[16]{0:T(128)} %prior.1, bf16[2,16,1024]{2,1,0:T(8,128)(2,1)} %q_hbm.1, bf16[2,16,256]{2,1,0:T(8,128)(2,1)} %new_hbm.1, ...), custom_call_target="tpu_custom_call" | custom-call | tf_op jit(solution)/shard_map/smc_step/pallas_call | solution.py:377
  35.0 0.0 copy-start
  35.1 1.2 %copy.18 = f32[2,16]{1,0:T(2,128)} copy(f32[2,16]{1,0:T(2,128)} %get-tuple-element.16) | data formatting | bytes 256
  36.3 1.2 %copy.19 = f32[16]{0:T(128)} copy(f32[16]{0:T(128)} %bitcast.5) | data formatting | bytes 128
  37.5 2.3 %copy.20 = bf16[16,128,256]{2,1,0:T(8,128)(2,1)} copy(bf16[16,128,256]{2,1,0:T(8,128)(2,1)} %get-tuple-element.18) | data formatting | bytes 2097152
  39.7 0.0 copy-done
  39.7 0.5 %copy.21 = s32[16]{0:T(128)} copy(s32[16]{0:T(128)S(1)} %copy-done) | data formatting | bytes 128
Async XLA Ops:
  35.0 4.7 %copy-start = (s32[16]{0:T(128)S(1)}, s32[16]{0:T(128)}, u32[]{:S(2)}) copy-start(s32[16]{0:T(128)} %get-tuple-element.19) | copy-start | bytes 196

commit v2 on v1

v2 whole, which is shorter than its diff:
```python
import functools
import math

import jax
import jax.numpy as jnp
from jax import lax
from jax.experimental import pallas as pl
from jax.experimental.pallas import tpu as pltpu
from jax.sharding import PartitionSpec as P

HEAD_DIM = 128
Y_DIM = 4
NEG_FILL = -1e30
MESH = pl.DeviceIdType.MESH
LOG2E = 1.4426950408889634
PARTS = 4
OFFSETS = (2, 1, -2, -1)


def kernel(
    sizes,
    anc_hbm,
    lens_hbm,
    toks_hbm,
    prior_hbm,
    q_hbm,
    new_hbm,
    gen_hbm,
    prompt_hbm,
    tv_hbm,
    bias_hbm,
    twist_out,
    norm_out,
    cache_out,
    len_out,
    anc,
    lens,
    toks,
    prior,
    qv,
    newv,
    cache,
    keyv,
    valv,
    tvv,
    biasv,
    scores,
    picked,
    relay,
    landed,
    bias_rows,
    plane_rows,
    z_rows,
    small_sems,
    in_sems,
    key_sems,
    val_sems,
    hop_send,
    hop_recv,
    plane_send,
    plane_recv,
    z_send,
    z_recv,
    below_sem,
    above_sem,
):
    n_dom, n_tp, per_dev, gen, prompt_len, group = sizes
    n_z = n_dom // Y_DIM
    n_plane = n_tp * Y_DIM
    dom = lax.axis_index("dom")
    tp = lax.axis_index("tp")
    my_y = lax.rem(dom, Y_DIM)
    my_z = dom // Y_DIM
    base = dom * per_dev
    bias_len = bias_hbm.shape[0]
    bias_part = biasv.shape[0]
    bias_last = bias_len - (n_tp - 1) * bias_part
    key_part = prompt_len // PARTS

    def device(d, t):
        return {"dom": d, "tp": t}

    def signal(sem, target):
        pl.semaphore_signal(sem, inc=1, device_id=target, device_id_type=MESH)

    def z_device(z):
        return device(z * Y_DIM + my_y, tp)

    def plane_peer(k):
        slot = lax.rem(tp * Y_DIM + my_y + k, n_plane)
        return slot, device(my_z * Y_DIM + lax.rem(slot, Y_DIM), slot // Y_DIM)

    copy = pltpu.make_async_copy
    load_q = copy(q_hbm, qv, in_sems.at[0])
    load_gen = copy(gen_hbm, cache, in_sems.at[1])
    load_new = copy(new_hbm, newv, in_sems.at[2])
    load_tv = copy(tv_hbm, tvv, in_sems.at[3])
    load_keys = [
        copy(
            prompt_hbm.at[c * key_part : (c + 1) * key_part, 0:HEAD_DIM],
            keyv.at[c * key_part : (c + 1) * key_part],
            key_sems.at[c],
        )
        for c in range(PARTS)
    ]
    load_vals = [
        copy(
            prompt_hbm.at[c * key_part : (c + 1) * key_part, HEAD_DIM : 2 * HEAD_DIM],
            valv.at[c * key_part : (c + 1) * key_part],
            val_sems.at[c],
        )
        for c in range(PARTS)
    ]
    load_anc = copy(anc_hbm, anc, small_sems.at[0])
    load_lens = copy(lens_hbm, lens, small_sems.at[1])
    load_toks = copy(toks_hbm, toks, small_sems.at[2])
    load_prior = copy(prior_hbm, prior, small_sems.at[3])
    bias_most = copy(
        bias_hbm.at[pl.ds(pl.multiple_of(tp * bias_part, 8), bias_part)], biasv, small_sems.at[4]
    )
    bias_rest = copy(
        bias_hbm.at[bias_len - bias_last : bias_len], biasv.at[0:bias_last], small_sems.at[4]
    )
    load_q.start()
    for item in load_keys:
        item.start()
    load_toks.start()
    load_lens.start()

    @pl.when(tp < n_tp - 1)
    def _():
        bias_most.start()

    @pl.when(tp == n_tp - 1)
    def _():
        bias_rest.start()

    load_gen.start()
    load_new.start()
    for item in load_vals:
        item.start()
    load_tv.start()
    load_prior.start()
    load_anc.start()

    barrier = pltpu.get_barrier_semaphore()

    def greet_plane(k, carry):
        signal(barrier, plane_peer(k)[1])
        return carry

    lax.fori_loop(1, n_plane, greet_plane, 0)

    @pl.when(dom < n_dom - 1)
    def _():
        signal(barrier, device(dom + 1, tp))

    @pl.when(dom > 0)
    def _():
        signal(barrier, device(dom - 1, tp))

    @pl.when(my_z < n_z - 1)
    def _():
        signal(barrier, z_device(my_z + 1))

    @pl.when(my_z > 0)
    def _():
        signal(barrier, z_device(my_z - 1))

    n_rows = 2 * group * per_dev
    to_row = lax.broadcasted_iota(jnp.int32, (n_rows, n_rows), 0)
    from_row = lax.broadcasted_iota(jnp.int32, (n_rows, n_rows), 1)
    wanted = lax.rem(to_row, 2 * group) * per_dev + to_row // (2 * group)
    order = jnp.where(from_row == wanted, 1.0, 0.0).astype(jnp.bfloat16)
    load_q.wait()
    tiles = [qv[t, :, h * HEAD_DIM : (h + 1) * HEAD_DIM] for t in range(2) for h in range(group)]
    stacked = jnp.concatenate(tiles, axis=0)
    query = jnp.dot(order, stacked, preferred_element_type=jnp.float32).astype(jnp.bfloat16)

    load_toks.wait()

    @pl.when(tp < n_tp - 1)
    def _():
        bias_most.wait()

    @pl.when(tp == n_tp - 1)
    def _():
        bias_rest.wait()

    lanes = lax.broadcasted_iota(jnp.int32, (1, 128), 1)
    for p in range(per_dev):
        for t in range(2):
            token = toks[t, p]
            spot = token // 128 - tp * bias_part
            held = jnp.logical_and(spot >= 0, spot < bias_part)
            lane = jnp.where(held, lax.rem(token, 128), -1)
            row = biasv[pl.ds(jnp.clip(spot, 0, bias_part - 1), 1), :]
            bias_rows[p * 2 + t : p * 2 + t + 1, :] = jnp.where(lanes == lane, row, 0.0)

    nt = (((1,), (1,)), ((), ()))
    part = 2 * group
    chunk = 512
    top = None
    for c in range(prompt_len // chunk):
        if c * chunk % key_part == 0:
            load_keys[c * chunk // key_part].wait()
        raw = lax.dot_general(
            query, keyv[c * chunk : (c + 1) * chunk, :], nt, preferred_element_type=jnp.float32
        )
        scores[:, c * chunk : (c + 1) * chunk] = raw
        for i in range(chunk // 128):
            piece = raw[:, i * 128 : (i + 1) * 128]
            top = piece if top is None else jnp.maximum(top, piece)

    load_lens.wait()
    load_new.wait()
    load_gen.wait()
    rows = lax.broadcasted_iota(jnp.int32, (gen, 2 * HEAD_DIM), 0)
    for p in range(per_dev):
        start = lens[base + p]
        first = newv[0, pl.ds(p, 1), :].astype(jnp.float32)
        second = newv[1, pl.ds(p, 1), :].astype(jnp.float32)
        kept = cache[p].astype(jnp.float32)
        later = jnp.where(rows == start + 1, second, 0.0)
        grown = jnp.where(rows < start, kept, jnp.where(rows == start, first, later))
        cache[p] = grown.astype(jnp.bfloat16)

    own = []
    cols = lax.broadcasted_iota(jnp.int32, (part, gen), 1)
    step = lax.broadcasted_iota(jnp.int32, (part, gen), 0) // group
    for p in range(per_dev):
        raw = lax.dot_general(
            query[p * part : (p + 1) * part], cache[p, :, 0:HEAD_DIM], nt,
            preferred_element_type=jnp.float32,
        )
        own.append(jnp.where(cols <= lens[base + p] + step, raw, NEG_FILL))
    own = jnp.concatenate(own, axis=0)
    row_max = jnp.max(jnp.maximum(top, own), axis=1, keepdims=True)
    scale = LOG2E / math.sqrt(HEAD_DIM)
    exps = jnp.exp2((own - row_max) * scale)
    total = exps
    probs = exps.astype(jnp.bfloat16)
    mixed = []
    for p in range(per_dev):
        mixed.append(
            jnp.dot(
                probs[p * part : (p + 1) * part], cache[p, :, HEAD_DIM : 2 * HEAD_DIM],
                preferred_element_type=jnp.float32,
            )
        )
    mixed = jnp.concatenate(mixed, axis=0)
    for c in range(prompt_len // chunk):
        if c * chunk % key_part == 0:
            load_vals[c * chunk // key_part].wait()
        exps = jnp.exp2((scores[:, c * chunk : (c + 1) * chunk] - row_max) * scale)
        for i in range(chunk // 128):
            total = total + exps[:, i * 128 : (i + 1) * 128]
        mixed = mixed + jnp.dot(
            exps.astype(jnp.bfloat16), valv[c * chunk : (c + 1) * chunk, :],
            preferred_element_type=jnp.float32,
        )
    row_sum = jnp.sum(total, axis=1, keepdims=True)
    mixed = mixed / row_sum
    load_tv.wait()
    weighted = mixed.reshape(2 * per_dev, group, HEAD_DIM) * tvv[...][None]
    pair_rows = jnp.sum(weighted, axis=1) + bias_rows[...]
    pair_col = jnp.sum(pair_rows, axis=1, keepdims=True)
    pair_ids = lax.broadcasted_iota(jnp.int32, (2 * per_dev, 128), 0)
    lane_ids = lax.broadcasted_iota(jnp.int32, (2 * per_dev, 128), 1)
    at_lane = lane_ids == lax.rem(pair_ids, 2) * per_dev + pair_ids // 2
    message = jnp.sum(jnp.where(at_lane, pair_col, 0.0), axis=0, keepdims=True)
    first_tp = jnp.where(tp == 0, 1.0, 0.0)
    load_prior.wait()
    for p in range(per_dev):
        message = jnp.where(lanes == 2 * per_dev + p, prior[p] * first_tp, message)
    me = tp * Y_DIM + my_y
    plane_rows[me] = message

    around = lambda count, top: (count > 0).astype(jnp.int32) + (count < top - 1).astype(jnp.int32)
    pl.semaphore_wait(barrier, n_plane - 1 + around(dom, n_dom) + around(my_z, n_z))

    def plane_copy(src, dst, peer):
        return pltpu.make_async_remote_copy(
            src_ref=plane_rows.at[src],
            dst_ref=plane_rows.at[dst],
            send_sem=plane_send.at[peer[0]],
            recv_sem=plane_recv.at[dst],
            device_id=peer[1],
            device_id_type=MESH,
        )

    def plane_start(k, carry):
        plane_copy(me, me, plane_peer(k)).start()
        return carry

    lax.fori_loop(1, n_plane, plane_start, 0)

    load_anc.wait()
    for slot, offset in enumerate(OFFSETS):
        target = jnp.clip(dom + offset, 0, n_dom - 1) * per_dev
        low, high = per_dev - 1, 0
        for i in range(per_dev):
            spot = anc[target + i] - base
            mine = jnp.logical_and(spot >= 0, spot < per_dev)
            low = jnp.minimum(low, jnp.where(mine, spot, per_dev - 1))
            high = jnp.maximum(high, jnp.where(mine, spot, 0))
        picked[slot, 0] = cache[low]
        picked[slot, 1] = cache[high]

    @pl.when(my_z > 0)
    def _():
        pl.semaphore_wait(below_sem, 1)

    @pl.when(my_z < n_z - 1)
    def _():
        signal(below_sem, z_device(my_z + 1))

    def greet_below(z, carry):
        signal(above_sem, z_device(z))
        return carry

    lax.fori_loop(0, my_z, greet_below, 0)

    def hop(src, dst, i, shift):
        return pltpu.make_async_remote_copy(
            src_ref=src,
            dst_ref=dst,
            send_sem=hop_send.at[i],
            recv_sem=hop_recv.at[i],
            device_id=device(jnp.clip(dom + shift, 0, n_dom - 1), tp),
            device_id_type=MESH,
        )

    far = n_dom - 1
    inner = jnp.logical_and(dom > 0, dom < far)
    hops = [
        (hop(picked.at[0], relay.at[0], 0, 1), dom < far - 1, inner),
        (hop(picked.at[2], relay.at[1], 1, -1), dom > 1, inner),
        (hop(picked.at[1], landed.at[1], 2, 1), dom < far, dom > 0),
        (hop(picked.at[3], landed.at[3], 3, -1), dom > 0, dom < far),
        (hop(relay.at[0], landed.at[0], 4, 1), inner, dom > 1),
        (hop(relay.at[1], landed.at[2], 5, -1), inner, dom < far - 1),
    ]

    def start_hop(i):
        pl.when(hops[i][1])(hops[i][0].start)

    def receive_hop(i):
        pl.when(hops[i][2])(hops[i][0].wait_recv)

    for i in range(4):
        start_hop(i)

    def plane_wait(k, carry):
        peer = plane_peer(k)
        plane_copy(me, peer[0], peer).wait()
        return carry

    lax.fori_loop(1, n_plane, plane_wait, 0)

    def summed(y):
        acc = plane_rows[y]
        for t in range(1, n_tp):
            acc = acc + plane_rows[t * Y_DIM + y]
        return acc

    def weights(acc):
        later = pltpu.roll(acc, 128 - per_dev, 1)
        given = pltpu.roll(acc, 128 - 2 * per_dev, 1)
        return jnp.where(lanes < per_dev, given + later - acc, NEG_FILL), later

    all_weights = jnp.concatenate([weights(summed(y))[0] for y in range(Y_DIM)], axis=0)
    z_max = jnp.max(jnp.max(all_weights, axis=1, keepdims=True), axis=0, keepdims=True)
    z_exp = jnp.exp(all_weights - z_max)
    z_sum = jnp.sum(jnp.sum(z_exp, axis=1, keepdims=True), axis=0, keepdims=True)
    z_rows[my_z, 0:1, :] = jnp.broadcast_to(z_max, (1, 128))
    z_rows[my_z, 1:2, :] = jnp.broadcast_to(z_sum, (1, 128))

    def z_copy(dst, z):
        return pltpu.make_async_remote_copy(
            src_ref=z_rows.at[my_z],
            dst_ref=z_rows.at[dst],
            send_sem=z_send.at[z],
            recv_sem=z_recv.at[dst],
            device_id=z_device(z),
            device_id_type=MESH,
        )

    def z_start(z, carry):
        z_copy(my_z, z).start()
        return carry

    lax.fori_loop(0, my_z, z_start, 0)

    receive_hop(0)
    start_hop(4)
    receive_hop(1)
    start_hop(5)

    @pl.when(my_z < n_z - 1)
    def _():
        pl.semaphore_wait(above_sem, n_z - 1 - my_z)

    lax.fori_loop(my_z + 1, n_z, z_start, 0)

    own_sum = summed(my_y)
    own_weight, own_later = weights(own_sum)
    twist_out[0:1, :] = own_sum[:, 0:per_dev]
    twist_out[1:2, :] = own_later[:, 0:per_dev]

    for i in range(2, 6):
        receive_hop(i)
    firsts = []
    for offset in OFFSETS:
        low = per_dev - 1
        for i in range(per_dev):
            spot = anc[base + i] - (base - offset * per_dev)
            theirs = jnp.logical_and(spot >= 0, spot < per_dev)
            low = jnp.minimum(low, jnp.where(theirs, spot, per_dev - 1))
        firsts.append(low)
    new_lens = jnp.zeros((1, 128), jnp.int32)
    for p in range(per_dev):
        new_lens = jnp.where(lanes == p, lens[anc[base + p]] + 2, new_lens)
        spot = anc[base + p] - base
        home = jnp.logical_and(spot >= 0, spot < per_dev)
        home_spot = jnp.clip(spot, 0, per_dev - 1)
        place = 0
        for slot, offset in enumerate(OFFSETS):
            there = spot + offset * per_dev
            theirs = jnp.logical_and(there >= 0, there < per_dev)
            second = jnp.where(there == firsts[slot], 0, 1)
            place = jnp.where(theirs, 2 * slot + second, place)
        moved = landed[place // 2, lax.rem(place, 2)]
        cache_out[p] = jnp.where(home, cache[home_spot], moved)
    len_out[...] = new_lens[:, 0:per_dev]

    def z_wait(k, carry):
        z = lax.rem(my_z + k, n_z)
        z_copy(z, z).wait()
        return carry

    lax.fori_loop(1, n_z, z_wait, 0)
    maxes = z_rows[:, 0, :]
    sums = z_rows[:, 1, :]
    largest = jnp.max(maxes, axis=0, keepdims=True)
    exp_total = jnp.sum(sums * jnp.exp(maxes - largest), axis=0, keepdims=True)
    normalized = own_weight - (largest + jnp.log(exp_total))
    norm_out[...] = normalized[:, 0:per_dev]

    for item, sends, _ in hops:
        pl.when(sends)(item.wait_send)


def finish(*refs):
    count = (len(refs) - 1) // 2
    copies = [
        pltpu.make_async_copy(refs[i], refs[count + i], refs[-1].at[i]) for i in range(count)
    ]
    for item in copies:
        item.start()
    for item in copies:
        item.wait()


def local(
    n_dom,
    n_tp,
    queries,
    new_kv,
    gen_cache,
    prompt_kv,
    lengths,
    ancestors,
    tokens,
    twist_vector,
    twist_bias,
    prior_weights,
):
    per_dev, gen, width = gen_cache.shape
    prompt_len = prompt_kv.shape[0]
    group = queries.shape[2] // HEAD_DIM
    n_rows = 2 * group * per_dev
    n_z = n_dom // Y_DIM
    n_plane = n_tp * Y_DIM
    bias_table = twist_bias.reshape(-1, 128)
    bias_part = -(-bias_table.shape[0] // (8 * n_tp)) * 8
    any_space = pl.BlockSpec(memory_space=pl.ANY)
    vmem = pl.BlockSpec(memory_space=pltpu.VMEM)
    f32, bf16, i32 = jnp.float32, jnp.bfloat16, jnp.int32
    dma = pltpu.SemaphoreType.DMA
    shapes = (((2, per_dev), f32), ((1, per_dev), f32), (gen_cache.shape, bf16), ((1, per_dev), i32))
    results = pl.pallas_call(
        functools.partial(kernel, (n_dom, n_tp, per_dev, gen, prompt_len, group)),
        out_shape=tuple(pltpu.VMEM(*shape) for shape in shapes),
        in_specs=[any_space] * 10,
        out_specs=(vmem,) * 4,
        scratch_shapes=[
            pltpu.SMEM(ancestors.shape, i32),
            pltpu.SMEM(lengths.shape, i32),
            pltpu.SMEM(tokens.shape, i32),
            pltpu.SMEM(prior_weights.shape, f32),
            pltpu.VMEM(queries.shape, bf16),
            pltpu.VMEM(new_kv.shape, bf16),
            pltpu.VMEM(gen_cache.shape, bf16),
            pltpu.VMEM((prompt_len, HEAD_DIM), bf16),
            pltpu.VMEM((prompt_len, HEAD_DIM), bf16),
            pltpu.VMEM((group, HEAD_DIM), f32),
            pltpu.VMEM((bias_part, 128), f32),
            pltpu.VMEM((n_rows, prompt_len), f32),
            pltpu.VMEM((4, 2, gen, width), bf16),
            pltpu.VMEM((2, 2, gen, width), bf16),
            pltpu.VMEM((4, 2, gen, width), bf16),
            pltpu.VMEM((2 * per_dev, 128), f32),
            pltpu.VMEM((n_plane, 1, 128), f32),
            pltpu.VMEM((n_z, 2, 128), f32),
            dma((5,)),
            dma((4,)),
            dma((PARTS,)),
            dma((PARTS,)),
            dma((6,)),
            dma((6,)),
            dma((n_plane,)),
            dma((n_plane,)),
            dma((n_z,)),
            dma((n_z,)),
            pltpu.SemaphoreType.REGULAR,
            pltpu.SemaphoreType.REGULAR,
        ],
        compiler_params=pltpu.CompilerParams(collective_id=0, has_side_effects=True),
        name="smc_step",
    )(
        ancestors,
        lengths,
        tokens,
        prior_weights,
        queries,
        new_kv,
        gen_cache,
        prompt_kv,
        twist_vector.reshape(group, HEAD_DIM),
        bias_table,
    )
    held = [pltpu.with_memory_space_constraint(x, pltpu.VMEM) for x in results]
    twist, normalized, resampled, new_lengths = pl.pallas_call(
        finish,
        out_shape=tuple(jax.ShapeDtypeStruct(*shape) for shape in shapes),
        in_specs=[any_space] * 4,
        out_specs=(any_space,) * 4,
        scratch_shapes=[dma((4,))],
        compiler_params=pltpu.CompilerParams(vmem_limit_bytes=4 << 20),
        name="finish",
    )(*held)
    return twist, normalized.reshape(per_dev), resampled, new_lengths.reshape(per_dev)


def solution(mesh):
    in_specs = (
        P(None, "dom", "tp"),
        P(None, "dom", "tp"),
        P("dom", None, "tp"),
        P(None, "tp"),
        P(),
        P(),
        P(None, "dom"),
        P("tp"),
        P(),
        P("dom"),
    )
    out_specs = (P(None, "dom"), P("dom"), P("dom", None, "tp"), P("dom"))
    return jax.shard_map(
        functools.partial(local, mesh.shape["dom"], mesh.shape["tp"]),
        mesh=mesh,
        in_specs=in_specs,
        out_specs=out_specs,
        check_vma=False,
    )
```

time: 40.5 us -> 36.2 us (0.89)
  the two profiles are of different devices: /device:TPU:1 before, /device:TPU:480 now
where the time goes in v2:
time: 36.2 us; the launch traced here: 36.1 us
  Pallas kernels  35.5 us (98%)
  between operations  0.64 us (2%)
    pallas_call x1, Pallas kernels, local(): pl.pallas_call(functools.partial(kernel, (n_dom, n_tp, per_dev, gen, prom...  34.5 us
    pallas_call x1, Pallas kernels, local(): pl.pallas_call(finish, out_shape=tuple((jax.ShapeDtypeStruct(*shape) for...  1.02 us

profile of v2, /device:TPU:480, one launch (start us, length us, event | category | flops | bytes accessed | tf_op | source)
XLA Modules:
  0.0 36.1 jit_solution(16996688268304792456)
XLA Ops:
  0.6 34.5 %smc_step.1 = (f32[2,16]{1,0:T(2,128)S(1)}, f32[1,16]{1,0:T(1,128)S(1)}, bf16[16,128,256]{2,1,0:T(8,128)(2,1)S(1)}, s32[1,16]{1,0:T(1,128)S(1)}) custom-call(s32[1024]{0:T(1024)} %anc_hbm.1, s32[1024]{0:T(1024)} %lens_hbm.1, s32[2,16]{1,0:T(2,128)} %toks_hbm.1, f32[16]{0:T(128)} %prior_hbm.1, bf16[2,16,1024]{2,1,0:T(8,128)(2,1)} %q_hbm.1, ...), custom_call_target="tpu_custom_call" | custom-call | tf_op jit(solution)/shard_map/smc_step/pallas_call | solution.py:492
  35.1 1.0 %finish.1 = (f32[2,16]{1,0:T(2,128)}, f32[1,16]{1,0:T(1,128)}, bf16[16,128,256]{2,1,0:T(8,128)(2,1)}, s32[1,16]{1,0:T(1,128)}) custom-call(f32[2,16]{1,0:T(2,128)S(1)} %get-tuple-element.12.refs_0_, f32[1,16]{1,0:T(1,128)S(1)} %get-tuple-element.13.refs_1_, bf16[16,128,256]{2,1,0:T(8,128)(2,1)S(1)} %get-tuple-element.14.refs_2_, ...), custom_call_target="tpu_custom_call" | custom-call | tf_op jit(solution)/shard_map/finish/pallas_call | solution.py:544

commit v3 on v2

--- a/solution.py
+++ b/solution.py
@@ -61,10 +61,11 @@
     plane_recv,
     z_send,
     z_recv,
-    below_sem,
+    next_sem,
     above_sem,
 ):
     n_dom, n_tp, per_dev, gen, prompt_len, group = sizes
+    f32, bf16 = jnp.float32, jnp.bfloat16
     n_z = n_dom // Y_DIM
     n_plane = n_tp * Y_DIM
     dom = lax.axis_index("dom")
@@ -86,9 +87,13 @@
     def z_device(z):
         return device(z * Y_DIM + my_y, tp)
 
-    def plane_peer(k):
-        slot = lax.rem(tp * Y_DIM + my_y + k, n_plane)
-        return slot, device(my_z * Y_DIM + lax.rem(slot, Y_DIM), slot // Y_DIM)
+    me = tp * Y_DIM + my_y
+
+    def plane_slot(k):
+        return lax.rem(me + k, n_plane)
+
+    def plane_device(slot):
+        return device(my_z * Y_DIM + lax.rem(slot, Y_DIM), slot // Y_DIM)
 
     copy = pltpu.make_async_copy
     load_q = copy(q_hbm, qv, in_sems.at[0])
@@ -146,26 +151,19 @@
     barrier = pltpu.get_barrier_semaphore()
 
     def greet_plane(k, carry):
-        signal(barrier, plane_peer(k)[1])
+        signal(barrier, plane_device(plane_slot(k)))
         return carry
 
+    def greet_above(z, carry):
+        signal(barrier, z_device(z))
+        return carry
+
     lax.fori_loop(1, n_plane, greet_plane, 0)
+    lax.fori_loop(my_z + 1, n_z, greet_above, 0)
 
     @pl.when(dom < n_dom - 1)
     def _():
         signal(barrier, device(dom + 1, tp))
-
-    @pl.when(dom > 0)
-    def _():
-        signal(barrier, device(dom - 1, tp))
-
-    @pl.when(my_z < n_z - 1)
-    def _():
-        signal(barrier, z_device(my_z + 1))
-
-    @pl.when(my_z > 0)
-    def _():
-        signal(barrier, z_device(my_z - 1))
 
     n_rows = 2 * group * per_dev
     to_row = lax.broadcasted_iota(jnp.int32, (n_rows, n_rows), 0)
@@ -215,15 +213,17 @@
     load_lens.wait()
     load_new.wait()
     load_gen.wait()
-    rows = lax.broadcasted_iota(jnp.int32, (gen, 2 * HEAD_DIM), 0)
+    rows = lax.broadcasted_iota(jnp.int32, (gen, 2 * HEAD_DIM), 0).astype(f32).astype(bf16)
     for p in range(per_dev):
-        start = lens[base + p]
-        first = newv[0, pl.ds(p, 1), :].astype(jnp.float32)
-        second = newv[1, pl.ds(p, 1), :].astype(jnp.float32)
-        kept = cache[p].astype(jnp.float32)
-        later = jnp.where(rows == start + 1, second, 0.0)
-        grown = jnp.where(rows < start, kept, jnp.where(rows == start, first, later))
-        cache[p] = grown.astype(jnp.bfloat16)
+        start = lens[base + p].astype(f32)
+        at_first = jnp.full((gen, 2 * HEAD_DIM), start, f32).astype(bf16)
+        at_second = jnp.full((gen, 2 * HEAD_DIM), start + 1.0, f32).astype(bf16)
+        first = jnp.broadcast_to(newv[0, pl.ds(p, 1), :], (gen, 2 * HEAD_DIM))
+        second = jnp.broadcast_to(newv[1, pl.ds(p, 1), :], (gen, 2 * HEAD_DIM))
+        later = jnp.where(rows == at_second, second, jnp.zeros_like(second))
+        cache[p] = jnp.where(
+            rows < at_first, cache[p], jnp.where(rows == at_first, first, later)
+        )
 
     own = []
     cols = lax.broadcasted_iota(jnp.int32, (part, gen), 1)
@@ -273,27 +273,43 @@
     load_prior.wait()
     for p in range(per_dev):
         message = jnp.where(lanes == 2 * per_dev + p, prior[p] * first_tp, message)
-    me = tp * Y_DIM + my_y
     plane_rows[me] = message
 
-    around = lambda count, top: (count > 0).astype(jnp.int32) + (count < top - 1).astype(jnp.int32)
-    pl.semaphore_wait(barrier, n_plane - 1 + around(dom, n_dom) + around(my_z, n_z))
-
-    def plane_copy(src, dst, peer):
+    pl.semaphore_wait(
+        barrier, n_plane - 1 + my_z + jnp.where(dom > 0, 1, 0)
+    )
+
+    n_x = n_tp // 2
+    my_x, core = tp // 2, lax.rem(tp, 2)
+    farthest = lambda n: sorted(range(n), key=lambda d: -min(d, n - d))
+    targets = []
+    for target_core in range(2):
+        for dx in farthest(n_x):
+            for dy in farthest(Y_DIM):
+                if dx or dy:
+                    targets.append((dx, dy, target_core))
+    targets.append((0, 0, 1 - core))
+
+    def plane_send_to(j):
+        dx, dy, target_core = targets[j]
+        x = lax.rem(my_x + dx, n_x)
+        y = lax.rem(my_y + dy, Y_DIM)
         return pltpu.make_async_remote_copy(
-            src_ref=plane_rows.at[src],
-            dst_ref=plane_rows.at[dst],
-            send_sem=plane_send.at[peer[0]],
-            recv_sem=plane_recv.at[dst],
-            device_id=peer[1],
+            src_ref=plane_rows.at[me],
+            dst_ref=plane_rows.at[me],
+            send_sem=plane_send.at[j],
+            recv_sem=plane_recv.at[me],
+            device_id=device(my_z * Y_DIM + y, x * 2 + target_core),
             device_id_type=MESH,
         )
 
-    def plane_start(k, carry):
-        plane_copy(me, me, plane_peer(k)).start()
-        return carry
-
-    lax.fori_loop(1, n_plane, plane_start, 0)
+    plane_sends = [plane_send_to(j) for j in range(len(targets))]
+    for item in plane_sends:
+        item.start()
+
+    @pl.when(dom > 0)
+    def _():
+        signal(next_sem, device(dom - 1, tp))
 
     load_anc.wait()
     for slot, offset in enumerate(OFFSETS):
@@ -307,13 +323,53 @@
         picked[slot, 0] = cache[low]
         picked[slot, 1] = cache[high]
 
-    @pl.when(my_z > 0)
-    def _():
-        pl.semaphore_wait(below_sem, 1)
-
-    @pl.when(my_z < n_z - 1)
-    def _():
-        signal(below_sem, z_device(my_z + 1))
+    def plane_wait(k, carry):
+        slot = plane_slot(k)
+        pltpu.make_async_remote_copy(
+            src_ref=plane_rows.at[slot],
+            dst_ref=plane_rows.at[slot],
+            send_sem=plane_send.at[0],
+            recv_sem=plane_recv.at[slot],
+            device_id=plane_device(slot),
+            device_id_type=MESH,
+        ).wait_recv()
+        return carry
+
+    lax.fori_loop(1, n_plane, plane_wait, 0)
+
+    def summed(y):
+        acc = plane_rows[y]
+        for t in range(1, n_tp):
+            acc = acc + plane_rows[t * Y_DIM + y]
+        return acc
+
+    def weights(acc):
+        later = pltpu.roll(acc, 128 - per_dev, 1)
+        given = pltpu.roll(acc, 128 - 2 * per_dev, 1)
+        return jnp.where(lanes < per_dev, given + later - acc, NEG_FILL), later
+
+    all_weights = jnp.concatenate([weights(summed(y))[0] for y in range(Y_DIM)], axis=0)
+    z_max = jnp.max(jnp.max(all_weights, axis=1, keepdims=True), axis=0, keepdims=True)
+    z_exp = jnp.exp(all_weights - z_max)
+    z_sum = jnp.sum(jnp.sum(z_exp, axis=1, keepdims=True), axis=0, keepdims=True)
+    z_rows[my_z, 0:1, :] = jnp.broadcast_to(z_max, (1, 128))
+    z_rows[my_z, 1:2, :] = jnp.broadcast_to(z_sum, (1, 128))
+
+    def z_copy(dst, z):
+        return pltpu.make_async_remote_copy(
+            src_ref=z_rows.at[my_z],
+            dst_ref=z_rows.at[dst],
+            send_sem=z_send.at[z],
+            recv_sem=z_recv.at[dst],
+            device_id=z_device(z),
+            device_id_type=MESH,
+        )
+
+    def z_start(z, carry):
+        z_copy(my_z, z).start()
+        return carry
+
+    lax.fori_loop(0, my_z, z_start, 0)
 
     def greet_below(z, carry):
         signal(above_sem, z_device(z))
@@ -348,49 +404,12 @@
     def receive_hop(i):
         pl.when(hops[i][2])(hops[i][0].wait_recv)
 
+    @pl.when(dom < far)
+    def _():
+        pl.semaphore_wait(next_sem, 1)
+
     for i in range(4):
         start_hop(i)
-
-    def plane_wait(k, carry):
-        peer = plane_peer(k)
-        plane_copy(me, peer[0], peer).wait()
-        return carry
-
-    lax.fori_loop(1, n_plane, plane_wait, 0)
-
-    def summed(y):
-        acc = plane_rows[y]
-        for t in range(1, n_tp):
-            acc = acc + plane_rows[t * Y_DIM + y]
-        return acc
-
-    def weights(acc):
-        later = pltpu.roll(acc, 128 - per_dev, 1)
-        given = pltpu.roll(acc, 128 - 2 * per_dev, 1)
-        return jnp.where(lanes < per_dev, given + later - acc, NEG_FILL), later
-
-    all_weights = jnp.concatenate([weights(summed(y))[0] for y in range(Y_DIM)], axis=0)
-    z_max = jnp.max(jnp.max(all_weights, axis=1, keepdims=True), axis=0, keepdims=True)
-    z_exp = jnp.exp(all_weights - z_max)
-    z_sum = jnp.sum(jnp.sum(z_exp, axis=1, keepdims=True), axis=0, keepdims=True)
-    z_rows[my_z, 0:1, :] = jnp.broadcast_to(z_max, (1, 128))
-    z_rows[my_z, 1:2, :] = jnp.broadcast_to(z_sum, (1, 128))
-
-    def z_copy(dst, z):
-        return pltpu.make_async_remote_copy(
-            src_ref=z_rows.at[my_z],
-            dst_ref=z_rows.at[dst],
-            send_sem=z_send.at[z],
-            recv_sem=z_recv.at[dst],
-            device_id=z_device(z),
-            device_id_type=MESH,
-        )
-
-    def z_start(z, carry):
-        z_copy(my_z, z).start()
-        return carry
-
-    lax.fori_loop(0, my_z, z_start, 0)
 
     receive_hop(0)
     start_hop(4)
@@ -449,6 +468,8 @@
 
     for item, sends, _ in hops:
         pl.when(sends)(item.wait_send)
+    for item in plane_sends:
+        item.wait_send()
 
 
 def finish(*refs):

time: 36.2 us -> 31.2 us (0.86)
  the two profiles are of different devices: /device:TPU:480 before, /device:TPU:1 now
where the time goes in v3:
time: 31.2 us; the launch traced here: 31.1 us
  Pallas kernels  30.4 us (97%)
  between operations  0.64 us (2%)
    pallas_call x1, Pallas kernels, local(): pl.pallas_call(functools.partial(kernel, (n_dom, n_tp, per_dev, gen, prom...  29.4 us
    pallas_call x1, Pallas kernels, local(): pl.pallas_call(finish, out_shape=tuple((jax.ShapeDtypeStruct(*shape) for...  1.02 us

profile of v3, /device:TPU:1, one launch (start us, length us, event | category | flops | bytes accessed | tf_op | source)
XLA Modules:
  0.0 31.1 jit_solution(16100715402537478457)
XLA Ops:
  0.6 29.4 %smc_step.1 = (f32[2,16]{1,0:T(2,128)S(1)}, f32[1,16]{1,0:T(1,128)S(1)}, bf16[16,128,256]{2,1,0:T(8,128)(2,1)S(1)}, s32[1,16]{1,0:T(1,128)S(1)}) custom-call(s32[1024]{0:T(1024)} %anc_hbm.1, s32[1024]{0:T(1024)} %lens_hbm.1, s32[2,16]{1,0:T(2,128)} %toks_hbm.1, f32[16]{0:T(128)} %prior_hbm.1, bf16[2,16,1024]{2,1,0:T(8,128)(2,1)} %q_hbm.1, ...), custom_call_target="tpu_custom_call" | custom-call | tf_op jit(solution)/shard_map/smc_step/pallas_call | solution.py:513
  30.1 1.0 %finish.1 = (f32[2,16]{1,0:T(2,128)}, f32[1,16]{1,0:T(1,128)}, bf16[16,128,256]{2,1,0:T(8,128)(2,1)}, s32[1,16]{1,0:T(1,128)}) custom-call(f32[2,16]{1,0:T(2,128)S(1)} %get-tuple-element.12.refs_0_, f32[1,16]{1,0:T(1,128)S(1)} %get-tuple-element.13.refs_1_, bf16[16,128,256]{2,1,0:T(8,128)(2,1)S(1)} %get-tuple-element.14.refs_2_, ...), custom_call_target="tpu_custom_call" | custom-call | tf_op jit(solution)/shard_map/finish/pallas_call | solution.py:565

commit v4 on v3

--- a/solution.py
+++ b/solution.py
@@ -126,26 +126,26 @@
     bias_rest = copy(
         bias_hbm.at[bias_len - bias_last : bias_len], biasv.at[0:bias_last], small_sems.at[4]
     )
+    load_toks.start()
+    load_prior.start()
+    load_lens.start()
     load_q.start()
+
+    @pl.when(tp < n_tp - 1)
+    def _():
+        bias_most.start()
+
+    @pl.when(tp == n_tp - 1)
+    def _():
+        bias_rest.start()
+
     for item in load_keys:
         item.start()
-    load_toks.start()
-    load_lens.start()
-
-    @pl.when(tp < n_tp - 1)
-    def _():
-        bias_most.start()
-
-    @pl.when(tp == n_tp - 1)
-    def _():
-        bias_rest.start()
-
+    load_new.start()
     load_gen.start()
-    load_new.start()
     for item in load_vals:
         item.start()
     load_tv.start()
-    load_prior.start()
     load_anc.start()
 
     barrier = pltpu.get_barrier_semaphore()
@@ -186,14 +186,30 @@
         bias_rest.wait()
 
     lanes = lax.broadcasted_iota(jnp.int32, (1, 128), 1)
+    bias_start = tp * (bias_part * 128)
     for p in range(per_dev):
         for t in range(2):
-            token = toks[t, p]
-            spot = token // 128 - tp * bias_part
-            held = jnp.logical_and(spot >= 0, spot < bias_part)
-            lane = jnp.where(held, lax.rem(token, 128), -1)
-            row = biasv[pl.ds(jnp.clip(spot, 0, bias_part - 1), 1), :]
-            bias_rows[p * 2 + t : p * 2 + t + 1, :] = jnp.where(lanes == lane, row, 0.0)
+            local_token = toks[t, p] - bias_start
+            spot = jnp.clip(lax.shift_right_arithmetic(local_token, 7), 0, bias_part - 1)
+            row = biasv[pl.ds(spot, 1), :]
+            bias_rows[p * 2 + t : p * 2 + t + 1, :] = jnp.where(
+                lanes == local_token - spot * 128, row, 0.0
+            )
+
+    first_tp = jnp.where(tp == 0, 1.0, 0.0)
+    load_prior.wait()
+    weight_lane = 2 * 2 * per_dev + per_dev * my_y
+    prior_row = jnp.zeros((1, 128), f32)
+    for p in range(per_dev):
+        prior_row = jnp.where(lanes == weight_lane + p, prior[p] * first_tp, prior_row)
+    pair_ids = lax.broadcasted_iota(jnp.int32, (2 * per_dev, 128), 0)
+    lane_ids = lax.broadcasted_iota(jnp.int32, (2 * per_dev, 128), 1)
+    pair_step = lax.rem(pair_ids, 2)
+    at_twist = lane_ids == pair_step * per_dev + pair_ids // 2
+    at_weight = lane_ids == weight_lane + pair_ids // 2
+    placed = jnp.where(
+        at_twist, 1.0, jnp.where(at_weight, (2 * pair_step - 1).astype(f32), 0.0)
+    )
 
     nt = (((1,), (1,)), ((), ()))
     part = 2 * group
@@ -212,33 +228,34 @@
 
     load_lens.wait()
     load_new.wait()
+    filler = jnp.zeros((128 - 2 * per_dev, HEAD_DIM), bf16)
+    new_keys = jnp.concatenate([newv[0, :, 0:HEAD_DIM], newv[1, :, 0:HEAD_DIM], filler], axis=0)
+    new_vals = jnp.concatenate(
+        [newv[0, :, HEAD_DIM : 2 * HEAD_DIM], newv[1, :, HEAD_DIM : 2 * HEAD_DIM], filler], axis=0
+    )
+    new_row = lax.broadcasted_iota(jnp.int32, (n_rows, 128), 0)
+    new_col = lax.broadcasted_iota(jnp.int32, (n_rows, 128), 1)
+    shown = jnp.logical_and(
+        lax.rem(new_col, per_dev) == new_row // (2 * group),
+        new_col // per_dev <= lax.rem(new_row // group, 2),
+    )
+    fresh = lax.dot_general(query, new_keys, nt, preferred_element_type=f32)
+    fresh = jnp.where(shown, fresh, NEG_FILL)
     load_gen.wait()
-    rows = lax.broadcasted_iota(jnp.int32, (gen, 2 * HEAD_DIM), 0).astype(f32).astype(bf16)
-    for p in range(per_dev):
-        start = lens[base + p].astype(f32)
-        at_first = jnp.full((gen, 2 * HEAD_DIM), start, f32).astype(bf16)
-        at_second = jnp.full((gen, 2 * HEAD_DIM), start + 1.0, f32).astype(bf16)
-        first = jnp.broadcast_to(newv[0, pl.ds(p, 1), :], (gen, 2 * HEAD_DIM))
-        second = jnp.broadcast_to(newv[1, pl.ds(p, 1), :], (gen, 2 * HEAD_DIM))
-        later = jnp.where(rows == at_second, second, jnp.zeros_like(second))
-        cache[p] = jnp.where(
-            rows < at_first, cache[p], jnp.where(rows == at_first, first, later)
-        )
-
     own = []
     cols = lax.broadcasted_iota(jnp.int32, (part, gen), 1)
-    step = lax.broadcasted_iota(jnp.int32, (part, gen), 0) // group
     for p in range(per_dev):
         raw = lax.dot_general(
             query[p * part : (p + 1) * part], cache[p, :, 0:HEAD_DIM], nt,
             preferred_element_type=jnp.float32,
         )
-        own.append(jnp.where(cols <= lens[base + p] + step, raw, NEG_FILL))
+        own.append(jnp.where(cols < lens[base + p], raw, NEG_FILL))
     own = jnp.concatenate(own, axis=0)
-    row_max = jnp.max(jnp.maximum(top, own), axis=1, keepdims=True)
+    row_max = jnp.max(jnp.maximum(jnp.maximum(top, fresh), own), axis=1, keepdims=True)
     scale = LOG2E / math.sqrt(HEAD_DIM)
     exps = jnp.exp2((own - row_max) * scale)
-    total = exps
+    fresh_exps = jnp.exp2((fresh - row_max) * scale)
+    total = exps + fresh_exps
     probs = exps.astype(jnp.bfloat16)
     mixed = []
     for p in range(per_dev):
@@ -248,31 +265,33 @@
                 preferred_element_type=jnp.float32,
             )
         )
-    mixed = jnp.concatenate(mixed, axis=0)
-    for c in range(prompt_len // chunk):
-        if c * chunk % key_part == 0:
-            load_vals[c * chunk // key_part].wait()
-        exps = jnp.exp2((scores[:, c * chunk : (c + 1) * chunk] - row_max) * scale)
-        for i in range(chunk // 128):
-            total = total + exps[:, i * 128 : (i + 1) * 128]
-        mixed = mixed + jnp.dot(
-            exps.astype(jnp.bfloat16), valv[c * chunk : (c + 1) * chunk, :],
-            preferred_element_type=jnp.float32,
-        )
+    mixed = jnp.concatenate(mixed, axis=0) + jnp.dot(
+        fresh_exps.astype(bf16), new_vals, preferred_element_type=f32
+    )
+    for item in load_vals:
+        item.wait()
+    block = n_rows // 2
+    totals, mixes = [], []
+    for r in range(2):
+        lines = slice(r * block, (r + 1) * block)
+        part_total, part_mixed = total[lines], mixed[lines]
+        for c in range(prompt_len // chunk):
+            exps = jnp.exp2((scores[lines, c * chunk : (c + 1) * chunk] - row_max[lines]) * scale)
+            for i in range(chunk // 128):
+                part_total = part_total + exps[:, i * 128 : (i + 1) * 128]
+            part_mixed = part_mixed + jnp.dot(
+                exps.astype(bf16), valv[c * chunk : (c + 1) * chunk, :], preferred_element_type=f32
+            )
+        totals.append(part_total)
+        mixes.append(part_mixed)
+    total, mixed = jnp.concatenate(totals, axis=0), jnp.concatenate(mixes, axis=0)
     row_sum = jnp.sum(total, axis=1, keepdims=True)
     mixed = mixed / row_sum
     load_tv.wait()
     weighted = mixed.reshape(2 * per_dev, group, HEAD_DIM) * tvv[...][None]
     pair_rows = jnp.sum(weighted, axis=1) + bias_rows[...]
     pair_col = jnp.sum(pair_rows, axis=1, keepdims=True)
-    pair_ids = lax.broadcasted_iota(jnp.int32, (2 * per_dev, 128), 0)
-    lane_ids = lax.broadcasted_iota(jnp.int32, (2 * per_dev, 128), 1)
-    at_lane = lane_ids == lax.rem(pair_ids, 2) * per_dev + pair_ids // 2
-    message = jnp.sum(jnp.where(at_lane, pair_col, 0.0), axis=0, keepdims=True)
-    first_tp = jnp.where(tp == 0, 1.0, 0.0)
-    load_prior.wait()
-    for p in range(per_dev):
-        message = jnp.where(lanes == 2 * per_dev + p, prior[p] * first_tp, message)
+    message = jnp.sum(placed * pair_col, axis=0, keepdims=True) + prior_row
     plane_rows[me] = message
 
     pl.semaphore_wait(
@@ -311,6 +330,18 @@
     def _():
         signal(next_sem, device(dom - 1, tp))
 
+    rows = lax.broadcasted_iota(jnp.int32, (gen, 2 * HEAD_DIM), 0).astype(f32).astype(bf16)
+    for p in range(per_dev):
+        start = lens[base + p].astype(f32)
+        at_first = jnp.full((gen, 2 * HEAD_DIM), start, f32).astype(bf16)
+        at_second = jnp.full((gen, 2 * HEAD_DIM), start + 1.0, f32).astype(bf16)
+        first = jnp.broadcast_to(newv[0, pl.ds(p, 1), :], (gen, 2 * HEAD_DIM))
+        second = jnp.broadcast_to(newv[1, pl.ds(p, 1), :], (gen, 2 * HEAD_DIM))
+        later = jnp.where(rows == at_second, second, jnp.zeros_like(second))
+        cache[p] = jnp.where(
+            rows < at_first, cache[p], jnp.where(rows == at_first, first, later)
+        )
+
     load_anc.wait()
     for slot, offset in enumerate(OFFSETS):
         target = jnp.clip(dom + offset, 0, n_dom - 1) * per_dev
@@ -323,8 +354,10 @@
         picked[slot, 0] = cache[low]
         picked[slot, 1] = cache[high]
 
-    def plane_wait(k, carry):
-        slot = plane_slot(k)
+    def plane_wait(dx, dy, source_core):
+        x = lax.rem(my_x + dx, n_x)
+        y = lax.rem(my_y + dy, Y_DIM)
+        slot = (x * 2 + source_core) * Y_DIM + y
         pltpu.make_async_remote_copy(
             src_ref=plane_rows.at[slot],
             dst_ref=plane_rows.at[slot],
@@ -333,27 +366,11 @@
             device_id=plane_device(slot),
             device_id_type=MESH,
         ).wait_recv()
-        return carry
-
-    lax.fori_loop(1, n_plane, plane_wait, 0)
-
-    def summed(y):
-        acc = plane_rows[y]
-        for t in range(1, n_tp):
-            acc = acc + plane_rows[t * Y_DIM + y]
-        return acc
-
-    def weights(acc):
-        later = pltpu.roll(acc, 128 - per_dev, 1)
-        given = pltpu.roll(acc, 128 - 2 * per_dev, 1)
-        return jnp.where(lanes < per_dev, given + later - acc, NEG_FILL), later
-
-    all_weights = jnp.concatenate([weights(summed(y))[0] for y in range(Y_DIM)], axis=0)
-    z_max = jnp.max(jnp.max(all_weights, axis=1, keepdims=True), axis=0, keepdims=True)
-    z_exp = jnp.exp(all_weights - z_max)
-    z_sum = jnp.sum(jnp.sum(z_exp, axis=1, keepdims=True), axis=0, keepdims=True)
-    z_rows[my_z, 0:1, :] = jnp.broadcast_to(z_max, (1, 128))
-    z_rows[my_z, 1:2, :] = jnp.broadcast_to(z_sum, (1, 128))
+
+    for target in reversed(targets):
+        plane_wait(*target)
+
+    z_rows[my_z] = jnp.sum(plane_rows[...], axis=0)
 
     def z_copy(dst, z):
         return pltpu.make_async_remote_copy(
@@ -422,10 +439,15 @@
 
     lax.fori_loop(my_z + 1, n_z, z_start, 0)
 
-    own_sum = summed(my_y)
-    own_weight, own_later = weights(own_sum)
+    own_sum = plane_rows[my_y]
+    for t in range(1, n_tp):
+        own_sum = own_sum + plane_rows[t * Y_DIM + my_y]
     twist_out[0:1, :] = own_sum[:, 0:per_dev]
-    twist_out[1:2, :] = own_later[:, 0:per_dev]
+    twist_out[1:2, :] = pltpu.roll(own_sum, 128 - per_dev, 1)[:, 0:per_dev]
+    own_weight = own_sum
+    for y in range(Y_DIM):
+        moved = pltpu.roll(own_sum, 128 - 4 * per_dev - y * per_dev, 1)
+        own_weight = jnp.where(my_y == y, moved, own_weight)
 
     for i in range(2, 6):
         receive_hop(i)
@@ -453,16 +475,12 @@
         cache_out[p] = jnp.where(home, cache[home_spot], moved)
     len_out[...] = new_lens[:, 0:per_dev]
 
-    def z_wait(k, carry):
+    for k in range(1, n_z):
         z = lax.rem(my_z + k, n_z)
-        z_copy(z, z).wait()
-        return carry
-
-    lax.fori_loop(1, n_z, z_wait, 0)
-    maxes = z_rows[:, 0, :]
-    sums = z_rows[:, 1, :]
-    largest = jnp.max(maxes, axis=0, keepdims=True)
-    exp_total = jnp.sum(sums * jnp.exp(maxes - largest), axis=0, keepdims=True)
+        z_copy(z, z).wait_recv()
+    all_weights = jnp.where((lanes >= 4 * per_dev)[None], z_rows[...], NEG_FILL)
+    largest = jnp.max(jnp.max(all_weights, axis=0), axis=1, keepdims=True)
+    exp_total = jnp.sum(jnp.sum(jnp.exp(all_weights - largest[None]), axis=0), axis=1, keepdims=True)
     normalized = own_weight - (largest + jnp.log(exp_total))
     norm_out[...] = normalized[:, 0:per_dev]
 
@@ -470,6 +488,9 @@
         pl.when(sends)(item.wait_send)
     for item in plane_sends:
         item.wait_send()
+    for k in range(1, n_z):
+        z = lax.rem(my_z + k, n_z)
+        z_copy(z, z).wait_send()
 
 
 def finish(*refs):
@@ -533,7 +554,7 @@
             pltpu.VMEM((4, 2, gen, width), bf16),
             pltpu.VMEM((2 * per_dev, 128), f32),
             pltpu.VMEM((n_plane, 1, 128), f32),
-            pltpu.VMEM((n_z, 2, 128), f32),
+            pltpu.VMEM((n_z, 1, 128), f32),
             dma((5,)),
             dma((4,)),
             dma((PARTS,)),

time: 31.2 us -> 30.8 us (0.987)
  Pallas kernels: 30.4 us -> 29.8 us
    pallas_call x1, Pallas kernels: 29.4 us -> 28.8 us  [local(): pl.pallas_call(functools.partial(kernel, (n_dom, n_tp, per_dev, gen, prom...]
where the time goes in v4:
time: 30.8 us; the launch traced here: 30.5 us
  Pallas kernels  29.8 us (97%)
  between operations  0.64 us (2%)
    pallas_call x1, Pallas kernels, local(): pl.pallas_call(functools.partial(kernel, (n_dom, n_tp, per_dev, gen, prom...  28.8 us
    pallas_call x1, Pallas kernels, local(): pl.pallas_call(finish, out_shape=tuple((jax.ShapeDtypeStruct(*shape) for...  1.02 us

profile of v4, /device:TPU:1, one launch (start us, length us, event | category | flops | bytes accessed | tf_op | source)
XLA Modules:
  0.0 30.5 jit_solution(18176235734123182778)
XLA Ops:
  0.6 28.8 %smc_step.1 = (f32[2,16]{1,0:T(2,128)S(1)}, f32[1,16]{1,0:T(1,128)S(1)}, bf16[16,128,256]{2,1,0:T(8,128)(2,1)S(1)}, s32[1,16]{1,0:T(1,128)S(1)}) custom-call(s32[1024]{0:T(1024)} %anc_hbm.1, s32[1024]{0:T(1024)} %lens_hbm.1, s32[2,16]{1,0:T(2,128)} %toks_hbm.1, f32[16]{0:T(128)} %prior_hbm.1, bf16[2,16,1024]{2,1,0:T(8,128)(2,1)} %q_hbm.1, ...), custom_call_target="tpu_custom_call" | custom-call | tf_op jit(solution)/shard_map/smc_step/pallas_call | solution.py:534
  29.5 1.0 %finish.1 = (f32[2,16]{1,0:T(2,128)}, f32[1,16]{1,0:T(1,128)}, bf16[16,128,256]{2,1,0:T(8,128)(2,1)}, s32[1,16]{1,0:T(1,128)}) custom-call(f32[2,16]{1,0:T(2,128)S(1)} %get-tuple-element.12.refs_0_, f32[1,16]{1,0:T(1,128)S(1)} %get-tuple-element.13.refs_1_, bf16[16,128,256]{2,1,0:T(8,128)(2,1)S(1)} %get-tuple-element.14.refs_2_, ...), custom_call_target="tpu_custom_call" | custom-call | tf_op jit(solution)/shard_map/finish/pallas_call | solution.py:586

commit v5 on v4

--- a/solution.py
+++ b/solution.py
@@ -13,7 +13,7 @@
 NEG_FILL = -1e30
 MESH = pl.DeviceIdType.MESH
 LOG2E = 1.4426950408889634
-PARTS = 4
+PARTS = 2
 OFFSETS = (2, 1, -2, -1)
 
 
@@ -54,7 +54,6 @@
     small_sems,
     in_sems,
     key_sems,
-    val_sems,
     hop_send,
     hop_recv,
     plane_send,
@@ -108,14 +107,7 @@
         )
         for c in range(PARTS)
     ]
-    load_vals = [
-        copy(
-            prompt_hbm.at[c * key_part : (c + 1) * key_part, HEAD_DIM : 2 * HEAD_DIM],
-            valv.at[c * key_part : (c + 1) * key_part],
-            val_sems.at[c],
-        )
-        for c in range(PARTS)
-    ]
+    load_vals = copy(prompt_hbm.at[:, HEAD_DIM : 2 * HEAD_DIM], valv, in_sems.at[4])
     load_anc = copy(anc_hbm, anc, small_sems.at[0])
     load_lens = copy(lens_hbm, lens, small_sems.at[1])
     load_toks = copy(toks_hbm, toks, small_sems.at[2])
@@ -142,11 +134,6 @@
     for item in load_keys:
         item.start()
     load_new.start()
-    load_gen.start()
-    for item in load_vals:
-        item.start()
-    load_tv.start()
-    load_anc.start()
 
     barrier = pltpu.get_barrier_semaphore()
 
@@ -164,6 +151,11 @@
     @pl.when(dom < n_dom - 1)
     def _():
         signal(barrier, device(dom + 1, tp))
+
+    load_gen.start()
+    load_vals.start()
+    load_tv.start()
+    load_anc.start()
 
     n_rows = 2 * group * per_dev
     to_row = lax.broadcasted_iota(jnp.int32, (n_rows, n_rows), 0)
@@ -228,6 +220,9 @@
 
     load_lens.wait()
     load_new.wait()
+    load_gen.wait()
+    load_vals.wait()
+    load_tv.wait()
     filler = jnp.zeros((128 - 2 * per_dev, HEAD_DIM), bf16)
     new_keys = jnp.concatenate([newv[0, :, 0:HEAD_DIM], newv[1, :, 0:HEAD_DIM], filler], axis=0)
     new_vals = jnp.concatenate(
@@ -241,7 +236,6 @@
     )
     fresh = lax.dot_general(query, new_keys, nt, preferred_element_type=f32)
     fresh = jnp.where(shown, fresh, NEG_FILL)
-    load_gen.wait()
     own = []
     cols = lax.broadcasted_iota(jnp.int32, (part, gen), 1)
     for p in range(per_dev):
@@ -268,8 +262,6 @@
     mixed = jnp.concatenate(mixed, axis=0) + jnp.dot(
         fresh_exps.astype(bf16), new_vals, preferred_element_type=f32
     )
-    for item in load_vals:
-        item.wait()
     block = n_rows // 2
     totals, mixes = [], []
     for r in range(2):
@@ -287,7 +279,6 @@
     total, mixed = jnp.concatenate(totals, axis=0), jnp.concatenate(mixes, axis=0)
     row_sum = jnp.sum(total, axis=1, keepdims=True)
     mixed = mixed / row_sum
-    load_tv.wait()
     weighted = mixed.reshape(2 * per_dev, group, HEAD_DIM) * tvv[...][None]
     pair_rows = jnp.sum(weighted, axis=1) + bias_rows[...]
     pair_col = jnp.sum(pair_rows, axis=1, keepdims=True)
@@ -316,8 +307,8 @@
         return pltpu.make_async_remote_copy(
             src_ref=plane_rows.at[me],
             dst_ref=plane_rows.at[me],
-            send_sem=plane_send.at[j],
-            recv_sem=plane_recv.at[me],
+            send_sem=plane_send,
+            recv_sem=plane_recv,
             device_id=device(my_z * Y_DIM + y, x * 2 + target_core),
             device_id_type=MESH,
         )
@@ -354,30 +345,27 @@
         picked[slot, 0] = cache[low]
         picked[slot, 1] = cache[high]
 
-    def plane_wait(dx, dy, source_core):
-        x = lax.rem(my_x + dx, n_x)
-        y = lax.rem(my_y + dy, Y_DIM)
-        slot = (x * 2 + source_core) * Y_DIM + y
-        pltpu.make_async_remote_copy(
-            src_ref=plane_rows.at[slot],
-            dst_ref=plane_rows.at[slot],
-            send_sem=plane_send.at[0],
-            recv_sem=plane_recv.at[slot],
-            device_id=plane_device(slot),
-            device_id_type=MESH,
-        ).wait_recv()
-
-    for target in reversed(targets):
-        plane_wait(*target)
-
-    z_rows[my_z] = jnp.sum(plane_rows[...], axis=0)
+    all_sent = pltpu.make_async_remote_copy(
+        src_ref=plane_rows.at[0 : n_plane - 1],
+        dst_ref=plane_rows.at[0 : n_plane - 1],
+        send_sem=plane_send,
+        recv_sem=plane_recv,
+        device_id=device(dom, 0),
+        device_id_type=MESH,
+    )
+    all_sent.wait_recv()
+
+    sums = [plane_rows[slot] for slot in range(n_plane)]
+    while len(sums) > 1:
+        sums = [a + b for a, b in zip(sums[::2], sums[1::2])]
+    z_rows[my_z] = sums[0]
 
     def z_copy(dst, z):
         return pltpu.make_async_remote_copy(
             src_ref=z_rows.at[my_z],
             dst_ref=z_rows.at[dst],
-            send_sem=z_send.at[z],
-            recv_sem=z_recv.at[dst],
+            send_sem=z_send,
+            recv_sem=z_recv,
             device_id=z_device(z),
             device_id_type=MESH,
         )
@@ -475,22 +463,24 @@
         cache_out[p] = jnp.where(home, cache[home_spot], moved)
     len_out[...] = new_lens[:, 0:per_dev]
 
-    for k in range(1, n_z):
-        z = lax.rem(my_z + k, n_z)
-        z_copy(z, z).wait_recv()
+    for item, sends, _ in hops:
+        pl.when(sends)(item.wait_send)
+    all_sent.wait_send()
+    z_all = pltpu.make_async_remote_copy(
+        src_ref=z_rows.at[0 : n_z - 1],
+        dst_ref=z_rows.at[0 : n_z - 1],
+        send_sem=z_send,
+        recv_sem=z_recv,
+        device_id=device(dom, 0),
+        device_id_type=MESH,
+    )
+    z_all.wait_send()
+    z_all.wait_recv()
     all_weights = jnp.where((lanes >= 4 * per_dev)[None], z_rows[...], NEG_FILL)
     largest = jnp.max(jnp.max(all_weights, axis=0), axis=1, keepdims=True)
     exp_total = jnp.sum(jnp.sum(jnp.exp(all_weights - largest[None]), axis=0), axis=1, keepdims=True)
     normalized = own_weight - (largest + jnp.log(exp_total))
     norm_out[...] = normalized[:, 0:per_dev]
-
-    for item, sends, _ in hops:
-        pl.when(sends)(item.wait_send)
-    for item in plane_sends:
-        item.wait_send()
-    for k in range(1, n_z):
-        z = lax.rem(my_z + k, n_z)
-        z_copy(z, z).wait_send()
 
 
 def finish(*refs):
@@ -556,15 +546,14 @@
             pltpu.VMEM((n_plane, 1, 128), f32),
             pltpu.VMEM((n_z, 1, 128), f32),
             dma((5,)),
-            dma((4,)),
-            dma((PARTS,)),
+            dma((5,)),
             dma((PARTS,)),
             dma((6,)),
             dma((6,)),
-            dma((n_plane,)),
-            dma((n_plane,)),
-            dma((n_z,)),
-            dma((n_z,)),
+            dma,
+            dma,
+            dma,
+            dma,
             pltpu.SemaphoreType.REGULAR,
             pltpu.SemaphoreType.REGULAR,
         ],

time: 30.8 us -> 29.6 us (0.961)
  Pallas kernels: 29.8 us -> 28.6 us
    pallas_call x1, Pallas kernels: 28.8 us -> 27.6 us  [local(): pl.pallas_call(functools.partial(kernel, (n_dom, n_tp, per_dev, gen, prom...]
where the time goes in v5:
time: 29.6 us; the launch traced here: 29.2 us
  Pallas kernels  28.6 us (97%)
  between operations  0.64 us (2%)
    pallas_call x1, Pallas kernels, local(): pl.pallas_call(functools.partial(kernel, (n_dom, n_tp, per_dev, gen, prom...  27.6 us
    pallas_call x1, Pallas kernels, local(): pl.pallas_call(finish, out_shape=tuple((jax.ShapeDtypeStruct(*shape) for...  1.02 us

profile of v5, /device:TPU:1, one launch (start us, length us, event | category | flops | bytes accessed | tf_op | source)
XLA Modules:
  0.0 29.2 jit_solution(3718379163058048973)
XLA Ops:
  0.6 27.6 %smc_step.1 = (f32[2,16]{1,0:T(2,128)S(1)}, f32[1,16]{1,0:T(1,128)S(1)}, bf16[16,128,256]{2,1,0:T(8,128)(2,1)S(1)}, s32[1,16]{1,0:T(1,128)S(1)}) custom-call(s32[1024]{0:T(1024)} %anc_hbm.1, s32[1024]{0:T(1024)} %lens_hbm.1, s32[2,16]{1,0:T(2,128)} %toks_hbm.1, f32[16]{0:T(128)} %prior_hbm.1, bf16[2,16,1024]{2,1,0:T(8,128)(2,1)} %q_hbm.1, ...), custom_call_target="tpu_custom_call" | custom-call | tf_op jit(solution)/shard_map/smc_step/pallas_call | solution.py:524
  28.2 1.0 %finish.1 = (f32[2,16]{1,0:T(2,128)}, f32[1,16]{1,0:T(1,128)}, bf16[16,128,256]{2,1,0:T(8,128)(2,1)}, s32[1,16]{1,0:T(1,128)}) custom-call(f32[2,16]{1,0:T(2,128)S(1)} %get-tuple-element.12.refs_0_, f32[1,16]{1,0:T(1,128)S(1)} %get-tuple-element.13.refs_1_, bf16[16,128,256]{2,1,0:T(8,128)(2,1)S(1)} %get-tuple-element.14.refs_2_, ...), custom_call_target="tpu_custom_call" | custom-call | tf_op jit(solution)/shard_map/finish/pallas_call | solution.py:575

commit v6 on v5

--- a/solution.py
+++ b/solution.py
@@ -88,12 +88,6 @@
 
     me = tp * Y_DIM + my_y
 
-    def plane_slot(k):
-        return lax.rem(me + k, n_plane)
-
-    def plane_device(slot):
-        return device(my_z * Y_DIM + lax.rem(slot, Y_DIM), slot // Y_DIM)
-
     copy = pltpu.make_async_copy
     load_q = copy(q_hbm, qv, in_sems.at[0])
     load_gen = copy(gen_hbm, cache, in_sems.at[1])
@@ -137,25 +131,40 @@
 
     barrier = pltpu.get_barrier_semaphore()
 
-    def greet_plane(k, carry):
-        signal(barrier, plane_device(plane_slot(k)))
-        return carry
-
-    def greet_above(z, carry):
-        signal(barrier, z_device(z))
-        return carry
-
-    lax.fori_loop(1, n_plane, greet_plane, 0)
-    lax.fori_loop(my_z + 1, n_z, greet_above, 0)
-
-    @pl.when(dom < n_dom - 1)
-    def _():
-        signal(barrier, device(dom + 1, tp))
+    n_x = n_tp // 2
+    my_x, core = tp // 2, lax.rem(tp, 2)
+    farthest = lambda n: sorted(range(n), key=lambda d: -min(d, n - d))
+    targets = []
+    for target_core in range(2):
+        for dx in farthest(n_x):
+            for dy in farthest(Y_DIM):
+                if dx or dy:
+                    targets.append((dx, dy, target_core))
+    targets.append((0, 0, 1 - core))
+
+    def plane_target(j):
+        dx, dy, target_core = targets[j]
+        x = lax.rem(my_x + dx, n_x)
+        y = lax.rem(my_y + dy, Y_DIM)
+        return device(my_z * Y_DIM + y, x * 2 + target_core)
+
+    for j in range(len(targets)):
+        signal(barrier, plane_target(j))
 
     load_gen.start()
     load_vals.start()
     load_tv.start()
     load_anc.start()
+
+    def greet_above(z, carry):
+        signal(barrier, z_device(z))
+        return carry
+
+    lax.fori_loop(my_z + 1, n_z, greet_above, 0)
+
+    @pl.when(dom < n_dom - 1)
+    def _():
+        signal(barrier, device(dom + 1, tp))
 
     n_rows = 2 * group * per_dev
     to_row = lax.broadcasted_iota(jnp.int32, (n_rows, n_rows), 0)
@@ -289,27 +298,13 @@
         barrier, n_plane - 1 + my_z + jnp.where(dom > 0, 1, 0)
     )
 
-    n_x = n_tp // 2
-    my_x, core = tp // 2, lax.rem(tp, 2)
-    farthest = lambda n: sorted(range(n), key=lambda d: -min(d, n - d))
-    targets = []
-    for target_core in range(2):
-        for dx in farthest(n_x):
-            for dy in farthest(Y_DIM):
-                if dx or dy:
-                    targets.append((dx, dy, target_core))
-    targets.append((0, 0, 1 - core))
-
     def plane_send_to(j):
-        dx, dy, target_core = targets[j]
-        x = lax.rem(my_x + dx, n_x)
-        y = lax.rem(my_y + dy, Y_DIM)
         return pltpu.make_async_remote_copy(
             src_ref=plane_rows.at[me],
             dst_ref=plane_rows.at[me],
             send_sem=plane_send,
             recv_sem=plane_recv,
-            device_id=device(my_z * Y_DIM + y, x * 2 + target_core),
+            device_id=plane_target(j),
             device_id_type=MESH,
         )
 

time: 29.6 us -> 29.3 us (0.990)
  Pallas kernels: 28.6 us -> 28.3 us
where the time goes in v6:
time: 29.3 us; the launch traced here: 29 us
  Pallas kernels  28.3 us (97%)
  between operations  0.64 us (2%)
    pallas_call x1, Pallas kernels, local(): pl.pallas_call(functools.partial(kernel, (n_dom, n_tp, per_dev, gen, prom...  27.3 us
    pallas_call x1, Pallas kernels, local(): pl.pallas_call(finish, out_shape=tuple((jax.ShapeDtypeStruct(*shape) for...  1.02 us

profile of v6, /device:TPU:1, one launch (start us, length us, event | category | flops | bytes accessed | tf_op | source)
XLA Modules:
  0.0 29.0 jit_solution(14977281496118256854)
XLA Ops:
  0.6 27.3 %smc_step.1 = (f32[2,16]{1,0:T(2,128)S(1)}, f32[1,16]{1,0:T(1,128)S(1)}, bf16[16,128,256]{2,1,0:T(8,128)(2,1)S(1)}, s32[1,16]{1,0:T(1,128)S(1)}) custom-call(s32[1024]{0:T(1024)} %anc_hbm.1, s32[1024]{0:T(1024)} %lens_hbm.1, s32[2,16]{1,0:T(2,128)} %toks_hbm.1, f32[16]{0:T(128)} %prior_hbm.1, bf16[2,16,1024]{2,1,0:T(8,128)(2,1)} %q_hbm.1, ...), custom_call_target="tpu_custom_call" | custom-call | tf_op jit(solution)/shard_map/smc_step/pallas_call | solution.py:519
  28.0 1.0 %finish.1 = (f32[2,16]{1,0:T(2,128)}, f32[1,16]{1,0:T(1,128)}, bf16[16,128,256]{2,1,0:T(8,128)(2,1)}, s32[1,16]{1,0:T(1,128)}) custom-call(f32[2,16]{1,0:T(2,128)S(1)} %get-tuple-element.12.refs_0_, f32[1,16]{1,0:T(1,128)S(1)} %get-tuple-element.13.refs_1_, bf16[16,128,256]{2,1,0:T(8,128)(2,1)S(1)} %get-tuple-element.14.refs_2_, ...), custom_call_target="tpu_custom_call" | custom-call | tf_op jit(solution)/shard_map/finish/pallas_call | solution.py:570

commit v7 on v6

--- a/solution.py
+++ b/solution.py
@@ -112,10 +112,12 @@
     bias_rest = copy(
         bias_hbm.at[bias_len - bias_last : bias_len], biasv.at[0:bias_last], small_sems.at[4]
     )
+    load_q.start()
+    for item in load_keys:
+        item.start()
     load_toks.start()
     load_prior.start()
     load_lens.start()
-    load_q.start()
 
     @pl.when(tp < n_tp - 1)
     def _():
@@ -125,8 +127,6 @@
     def _():
         bias_rest.start()
 
-    for item in load_keys:
-        item.start()
     load_new.start()
 
     barrier = pltpu.get_barrier_semaphore()
@@ -176,42 +176,6 @@
     stacked = jnp.concatenate(tiles, axis=0)
     query = jnp.dot(order, stacked, preferred_element_type=jnp.float32).astype(jnp.bfloat16)
 
-    load_toks.wait()
-
-    @pl.when(tp < n_tp - 1)
-    def _():
-        bias_most.wait()
-
-    @pl.when(tp == n_tp - 1)
-    def _():
-        bias_rest.wait()
-
-    lanes = lax.broadcasted_iota(jnp.int32, (1, 128), 1)
-    bias_start = tp * (bias_part * 128)
-    for p in range(per_dev):
-        for t in range(2):
-            local_token = toks[t, p] - bias_start
-            spot = jnp.clip(lax.shift_right_arithmetic(local_token, 7), 0, bias_part - 1)
-            row = biasv[pl.ds(spot, 1), :]
-            bias_rows[p * 2 + t : p * 2 + t + 1, :] = jnp.where(
-                lanes == local_token - spot * 128, row, 0.0
-            )
-
-    first_tp = jnp.where(tp == 0, 1.0, 0.0)
-    load_prior.wait()
-    weight_lane = 2 * 2 * per_dev + per_dev * my_y
-    prior_row = jnp.zeros((1, 128), f32)
-    for p in range(per_dev):
-        prior_row = jnp.where(lanes == weight_lane + p, prior[p] * first_tp, prior_row)
-    pair_ids = lax.broadcasted_iota(jnp.int32, (2 * per_dev, 128), 0)
-    lane_ids = lax.broadcasted_iota(jnp.int32, (2 * per_dev, 128), 1)
-    pair_step = lax.rem(pair_ids, 2)
-    at_twist = lane_ids == pair_step * per_dev + pair_ids // 2
-    at_weight = lane_ids == weight_lane + pair_ids // 2
-    placed = jnp.where(
-        at_twist, 1.0, jnp.where(at_weight, (2 * pair_step - 1).astype(f32), 0.0)
-    )
-
     nt = (((1,), (1,)), ((), ()))
     part = 2 * group
     chunk = 512
@@ -227,6 +191,17 @@
             piece = raw[:, i * 128 : (i + 1) * 128]
             top = piece if top is None else jnp.maximum(top, piece)
 
+    load_toks.wait()
+
+    @pl.when(tp < n_tp - 1)
+    def _():
+        bias_most.wait()
+
+    @pl.when(tp == n_tp - 1)
+    def _():
+        bias_rest.wait()
+
+    load_prior.wait()
     load_lens.wait()
     load_new.wait()
     load_gen.wait()
@@ -286,6 +261,31 @@
         totals.append(part_total)
         mixes.append(part_mixed)
     total, mixed = jnp.concatenate(totals, axis=0), jnp.concatenate(mixes, axis=0)
+    lanes = lax.broadcasted_iota(jnp.int32, (1, 128), 1)
+    bias_start = tp * (bias_part * 128)
+    for p in range(per_dev):
+        for t in range(2):
+            local_token = toks[t, p] - bias_start
+            spot = jnp.clip(lax.shift_right_arithmetic(local_token, 7), 0, bias_part - 1)
+            row = biasv[pl.ds(spot, 1), :]
+            bias_rows[p * 2 + t : p * 2 + t + 1, :] = jnp.where(
+                lanes == local_token - spot * 128, row, 0.0
+            )
+
+    first_tp = jnp.where(tp == 0, 1.0, 0.0)
+    weight_lane = 2 * 2 * per_dev + per_dev * my_y
+    prior_row = jnp.zeros((1, 128), f32)
+    for p in range(per_dev):
+        prior_row = jnp.where(lanes == weight_lane + p, prior[p] * first_tp, prior_row)
+    pair_ids = lax.broadcasted_iota(jnp.int32, (2 * per_dev, 128), 0)
+    lane_ids = lax.broadcasted_iota(jnp.int32, (2 * per_dev, 128), 1)
+    pair_step = lax.rem(pair_ids, 2)
+    at_twist = lane_ids == pair_step * per_dev + pair_ids // 2
+    at_weight = lane_ids == weight_lane + pair_ids // 2
+    placed = jnp.where(
+        at_twist, 1.0, jnp.where(at_weight, (2 * pair_step - 1).astype(f32), 0.0)
+    )
+
     row_sum = jnp.sum(total, axis=1, keepdims=True)
     mixed = mixed / row_sum
     weighted = mixed.reshape(2 * per_dev, group, HEAD_DIM) * tvv[...][None]

time: 29.3 us -> 29.3 us (level)
  no operation moved by 1% of the time
where the time goes in v7:
time: 29.3 us; the launch traced here: 28.9 us
  Pallas kernels  28.3 us (97%)
  between operations  0.64 us (2%)
    pallas_call x1, Pallas kernels, local(): pl.pallas_call(functools.partial(kernel, (n_dom, n_tp, per_dev, gen, prom...  27.2 us
    pallas_call x1, Pallas kernels, local(): pl.pallas_call(finish, out_shape=tuple((jax.ShapeDtypeStruct(*shape) for...  1.02 us

profile of v7, /device:TPU:1, one launch (start us, length us, event | category | flops | bytes accessed | tf_op | source)
XLA Modules:
  0.0 28.9 jit_solution(9878812189787565006)
XLA Ops:
  0.6 27.2 %smc_step.1 = (f32[2,16]{1,0:T(2,128)S(1)}, f32[1,16]{1,0:T(1,128)S(1)}, bf16[16,128,256]{2,1,0:T(8,128)(2,1)S(1)}, s32[1,16]{1,0:T(1,128)S(1)}) custom-call(s32[1024]{0:T(1024)} %anc_hbm.1, s32[1024]{0:T(1024)} %lens_hbm.1, s32[2,16]{1,0:T(2,128)} %toks_hbm.1, f32[16]{0:T(128)} %prior_hbm.1, bf16[2,16,1024]{2,1,0:T(8,128)(2,1)} %q_hbm.1, ...), custom_call_target="tpu_custom_call" | custom-call | tf_op jit(solution)/shard_map/smc_step/pallas_call | solution.py:519
  27.9 1.0 %finish.1 = (f32[2,16]{1,0:T(2,128)}, f32[1,16]{1,0:T(1,128)}, bf16[16,128,256]{2,1,0:T(8,128)(2,1)}, s32[1,16]{1,0:T(1,128)}) custom-call(f32[2,16]{1,0:T(2,128)S(1)} %get-tuple-element.12.refs_0_, f32[1,16]{1,0:T(1,128)S(1)} %get-tuple-element.13.refs_1_, bf16[16,128,256]{2,1,0:T(8,128)(2,1)S(1)} %get-tuple-element.14.refs_2_, ...), custom_call_target="tpu_custom_call" | custom-call | tf_op jit(solution)/shard_map/finish/pallas_call | solution.py:570

commit v8 on v7

--- a/solution.py
+++ b/solution.py
@@ -13,7 +13,7 @@
 NEG_FILL = -1e30
 MESH = pl.DeviceIdType.MESH
 LOG2E = 1.4426950408889634
-PARTS = 2
+PARTS = 1
 OFFSETS = (2, 1, -2, -1)
 
 

time: 29.3 us -> 29.3 us (level)
  no operation moved by 1% of the time
where the time goes in v8:
time: 29.3 us; the launch traced here: 29 us
  Pallas kernels  28.3 us (97%)
  between operations  0.64 us (2%)
    pallas_call x1, Pallas kernels, local(): pl.pallas_call(functools.partial(kernel, (n_dom, n_tp, per_dev, gen, prom...  27.3 us
    pallas_call x1, Pallas kernels, local(): pl.pallas_call(finish, out_shape=tuple((jax.ShapeDtypeStruct(*shape) for...  1.02 us

profile of v8, /device:TPU:1, one launch (start us, length us, event | category | flops | bytes accessed | tf_op | source)
XLA Modules:
  0.0 29.0 jit_solution(2786367432127777692)
XLA Ops:
  0.6 27.3 %smc_step.1 = (f32[2,16]{1,0:T(2,128)S(1)}, f32[1,16]{1,0:T(1,128)S(1)}, bf16[16,128,256]{2,1,0:T(8,128)(2,1)S(1)}, s32[1,16]{1,0:T(1,128)S(1)}) custom-call(s32[1024]{0:T(1024)} %anc_hbm.1, s32[1024]{0:T(1024)} %lens_hbm.1, s32[2,16]{1,0:T(2,128)} %toks_hbm.1, f32[16]{0:T(128)} %prior_hbm.1, bf16[2,16,1024]{2,1,0:T(8,128)(2,1)} %q_hbm.1, ...), custom_call_target="tpu_custom_call" | custom-call | tf_op jit(solution)/shard_map/smc_step/pallas_call | solution.py:519
  27.9 1.0 %finish.1 = (f32[2,16]{1,0:T(2,128)}, f32[1,16]{1,0:T(1,128)}, bf16[16,128,256]{2,1,0:T(8,128)(2,1)}, s32[1,16]{1,0:T(1,128)}) custom-call(f32[2,16]{1,0:T(2,128)S(1)} %get-tuple-element.12.refs_0_, f32[1,16]{1,0:T(1,128)S(1)} %get-tuple-element.13.refs_1_, bf16[16,128,256]{2,1,0:T(8,128)(2,1)S(1)} %get-tuple-element.14.refs_2_, ...), custom_call_target="tpu_custom_call" | custom-call | tf_op jit(solution)/shard_map/finish/pallas_call | solution.py:570

commit v9 on v7

--- a/solution.py
+++ b/solution.py
@@ -128,6 +128,10 @@
         bias_rest.start()
 
     load_new.start()
+    load_gen.start()
+    load_vals.start()
+    load_tv.start()
+    load_anc.start()
 
     barrier = pltpu.get_barrier_semaphore()
 
@@ -150,11 +154,6 @@
 
     for j in range(len(targets)):
         signal(barrier, plane_target(j))
-
-    load_gen.start()
-    load_vals.start()
-    load_tv.start()
-    load_anc.start()
 
     def greet_above(z, carry):
         signal(barrier, z_device(z))

time: 29.3 us -> 29.7 us (1.014)
  Pallas kernels: 28.3 us -> 28.7 us
    pallas_call x1, Pallas kernels: 27.2 us -> 27.6 us  [local(): pl.pallas_call(functools.partial(kernel, (n_dom, n_tp, per_dev, gen, prom...]
where the time goes in v9:
time: 29.7 us; the launch traced here: 29.3 us
  Pallas kernels  28.7 us (97%)
  between operations  0.64 us (2%)
    pallas_call x1, Pallas kernels, local(): pl.pallas_call(functools.partial(kernel, (n_dom, n_tp, per_dev, gen, prom...  27.6 us
    pallas_call x1, Pallas kernels, local(): pl.pallas_call(finish, out_shape=tuple((jax.ShapeDtypeStruct(*shape) for...  1.02 us

profile of v9, /device:TPU:1, one launch (start us, length us, event | category | flops | bytes accessed | tf_op | source)
XLA Modules:
  0.0 29.3 jit_solution(9003417643732157178)
XLA Ops:
  0.6 27.6 %smc_step.1 = (f32[2,16]{1,0:T(2,128)S(1)}, f32[1,16]{1,0:T(1,128)S(1)}, bf16[16,128,256]{2,1,0:T(8,128)(2,1)S(1)}, s32[1,16]{1,0:T(1,128)S(1)}) custom-call(s32[1024]{0:T(1024)} %anc_hbm.1, s32[1024]{0:T(1024)} %lens_hbm.1, s32[2,16]{1,0:T(2,128)} %toks_hbm.1, f32[16]{0:T(128)} %prior_hbm.1, bf16[2,16,1024]{2,1,0:T(8,128)(2,1)} %q_hbm.1, ...), custom_call_target="tpu_custom_call" | custom-call | tf_op jit(solution)/shard_map/smc_step/pallas_call | solution.py:518
  28.3 1.0 %finish.1 = (f32[2,16]{1,0:T(2,128)}, f32[1,16]{1,0:T(1,128)}, bf16[16,128,256]{2,1,0:T(8,128)(2,1)}, s32[1,16]{1,0:T(1,128)}) custom-call(f32[2,16]{1,0:T(2,128)S(1)} %get-tuple-element.12.refs_0_, f32[1,16]{1,0:T(1,128)S(1)} %get-tuple-element.13.refs_1_, bf16[16,128,256]{2,1,0:T(8,128)(2,1)S(1)} %get-tuple-element.14.refs_2_, ...), custom_call_target="tpu_custom_call" | custom-call | tf_op jit(solution)/shard_map/finish/pallas_call | solution.py:569
